TPU v7x, 1024 devices: a whole 4x4x32 slice. The times are simulated.
1024 devices in a mesh: seq: 32 (over z), pipe: 8 (over y, core), dp: 4 (over x).
Axes of the slice: x: 4, y: 4, z: 32, core: 2. Of those that a mesh axis runs over, the one named last changes fastest.
Arguments:
- saved_queries: bfloat16 [8, 4, 4096, 2048], P('pipe', 'dp', None, 'seq'), may hold values from -8 to 8
- saved_keys: bfloat16 [8, 4, 4096, 512], P('pipe', 'dp', 'seq'), may hold values from -8 to 8
- saved_values: bfloat16 [8, 4, 4096, 512], P('pipe', 'dp', 'seq'), may hold values from -6 to 6
- output_grad: bfloat16 [8, 4, 4096, 2048], P('pipe', 'dp', 'seq'), may hold values from -6 to 6
- rel_bias: float32 [8, 32, 256], P('pipe', 'seq'), may hold values from -4 to 4
- key_tiles: int32 [8, 32, 32, 4], P('pipe', 'seq'), may hold values from 0 to 31, as said below
- live_count: int32 [8, 32, 32], P('pipe', 'seq'), may hold values from 1 to 4
Outputs:
- carried_query_gradient: bfloat16 [8, 4, 4096, 2048], P('pipe', 'dp', 'seq')
- key_grad: bfloat16 [8, 4, 4096, 512], P('pipe', 'dp', 'seq')
- value_grad: bfloat16 [8, 4, 4096, 512], P('pipe', 'dp', 'seq')
- bias_grad: float32 [8, 32, 256], P('pipe', 'seq', 'dp')
Inputs may be any that keep to these rules, and one draw needn't show every extreme that they name: `key_tiles`: for each section, head and query tile i, slot 0 holds i, the first live_count slots name distinct key tiles no later than i, and the other slots hold i.
All inputs are finite; a program needn't handle non-finite values.
Results may differ from a plain program's by a relative error of at most 0.0085.
Values may be sent and summed in bfloat16 or wider, within the bound.
No kernel may reach another device: no remote copies, remote signals or barrier semaphores. Data moves between devices by JAX's collectives and lax.ppermute only.
A program may use at most 64 MiB of HBM per device.

v0:
```python
import jax
import jax.numpy as jnp
from jax import lax
from jax.sharding import PartitionSpec as P

HEADS = 32
KVH = 8
HD = 64
TILE = 128
BUCKET = 16
SLOTS = 4


neg_big = -1e30
full_precision = lax.Precision.HIGHEST


def passed_along(x, axis, by):
    devices = lax.axis_size(axis)
    pairs = [(i, i + by) for i in range(devices) if 0 <= i + by < devices]
    return lax.ppermute(x, axis, pairs)


def offset_table(offsets):
    row_ids = jnp.arange(TILE)[:, None]
    col_ids = jnp.arange(TILE)[None, :]
    offset_ids = ((row_ids - col_ids) // BUCKET + offsets).reshape(1, TILE * TILE)
    return (offset_ids == jnp.arange(2 * offsets)[:, None]).astype(jnp.float32)


def to_tiles(rows_in, local_heads):
    seq_len = rows_in.shape[0]
    return rows_in.reshape(seq_len // TILE, TILE, local_heads, HD).transpose(2, 0, 1, 3)


def from_tiles(tiles_in):
    local_heads, tiles_n = (tiles_in.shape[0], tiles_in.shape[1])
    return tiles_in.transpose(1, 2, 0, 3).reshape(tiles_n * TILE, local_heads * HD)


def attention_grads(
    queries, key_rows, value_rows, grad_rows, bias_rows, tile_list, live_slots, slot_top
):
    local_heads, tiles_n = (tile_list.shape[0], tile_list.shape[1])
    rel_count = bias_rows.shape[1]
    offsets = TILE // BUCKET
    logit_scale = HD ** (-0.5)
    query_blocks = to_tiles(queries, local_heads)
    grad_tiles = to_tiles(grad_rows, local_heads)
    key_all = to_tiles(key_rows, local_heads)
    value_all = to_tiles(value_rows, local_heads)
    off_table = offset_table(offsets)
    row_ids = jnp.arange(TILE)
    future = row_ids[None, :] > row_ids[:, None]
    tile_ids = jnp.arange(tiles_n)
    pick_tile = jax.vmap(lambda source, chosen: source[chosen])

    def slot_view(slot):
        key_ids = lax.dynamic_index_in_dim(tile_list, slot, 2, keepdims=False)
        live_mask = slot < live_slots
        current_key_block = pick_tile(key_all, key_ids)
        value_tile = pick_tile(value_all, key_ids)
        diagonal = key_ids == tile_ids[None, :]
        allowed = live_mask[:, :, None, None] & ~(diagonal[:, :, None, None] & future[None, None])
        distance_buckets = (
            (tile_ids[None, :] - key_ids)[..., None] * offsets + jnp.arange(2 * offsets) - offsets
        )
        bucket_pick = (
            jnp.clip(distance_buckets, 0, rel_count - 1)[..., None] == jnp.arange(rel_count)
        ).astype(jnp.float32)
        near_bias = jnp.einsum("hior,hr->hio", bucket_pick, bias_rows, precision=full_precision)
        bias_tile = jnp.einsum("hio,ox->hix", near_bias, off_table, precision=full_precision)
        bias_tile = bias_tile.reshape(local_heads, tiles_n, TILE, TILE)
        attention_logits = (
            logit_scale
            * jnp.einsum(
                "hiad,hibd->hiab",
                query_blocks,
                current_key_block,
                preferred_element_type=jnp.float32,
            )
            + bias_tile
        )
        attention_logits = jnp.where(allowed, attention_logits, neg_big)
        grad_prob = jnp.einsum(
            "hiac,hibc->hiab", grad_tiles, value_tile, preferred_element_type=jnp.float32
        )
        return (key_ids, allowed, current_key_block, attention_logits, grad_prob, bucket_pick)

    def first_pass(slot, state_in):
        row_max, row_sum, delta_sum = state_in
        key_ids, allowed, current_key_block, attention_logits, grad_prob, bucket_pick = slot_view(
            slot
        )
        new_max = jnp.maximum(row_max, jnp.max(attention_logits, axis=-1))
        rescale = jnp.exp(row_max - new_max)
        weights = jnp.where(allowed, jnp.exp(attention_logits - new_max[..., None]), 0.0)
        return (
            new_max,
            row_sum * rescale + jnp.sum(weights, axis=-1),
            delta_sum * rescale + jnp.sum(weights * grad_prob, axis=-1),
        )

    row_shape = (local_heads, tiles_n, TILE)
    initial = (
        jnp.full(row_shape, neg_big, jnp.float32),
        jnp.zeros(row_shape, jnp.float32),
        jnp.zeros(row_shape, jnp.float32),
    )
    row_max, row_sum, delta_sum = lax.fori_loop(0, slot_top, first_pass, initial)
    log_norm = row_max + jnp.log(row_sum)
    row_delta = delta_sum / row_sum

    def second_pass(slot, state_in):
        query_acc, key_acc, value_acc, bias_acc = state_in
        key_ids, allowed, current_key_block, attention_logits, grad_prob, bucket_pick = slot_view(
            slot
        )
        probs = jnp.where(allowed, jnp.exp(attention_logits - log_norm[..., None]), 0.0)
        probs_low = probs.astype(jnp.bfloat16)
        grad_score = probs * (grad_prob - row_delta[..., None])
        gradient_reduced = grad_score.astype(jnp.bfloat16)
        scatter_lookup = (key_ids[:, None, :] == tile_ids[None, :, None]).astype(jnp.float32)
        value_part = jnp.einsum(
            "hiab,hiac->hibc", probs_low, grad_tiles, preferred_element_type=jnp.float32
        )
        key_part = jnp.einsum(
            "hiab,hiad->hibd", gradient_reduced, query_blocks, preferred_element_type=jnp.float32
        )
        query_acc = query_acc + jnp.einsum(
            "hiab,hibd->hiad",
            gradient_reduced,
            current_key_block,
            preferred_element_type=jnp.float32,
        )
        key_acc = key_acc + jnp.einsum(
            "hki,hibd->hkbd", scatter_lookup, key_part, precision=full_precision
        )
        value_acc = value_acc + jnp.einsum(
            "hki,hibc->hkbc", scatter_lookup, value_part, precision=full_precision
        )
        spread = jnp.einsum(
            "hix,ox->hio",
            grad_score.reshape(local_heads, tiles_n, TILE * TILE),
            off_table,
            precision=full_precision,
        )
        bias_acc = bias_acc + jnp.einsum(
            "hio,hior->hr", spread, bucket_pick, precision=full_precision
        )
        return (query_acc, key_acc, value_acc, bias_acc)

    tile_shape = (local_heads, tiles_n, TILE, HD)
    initial = (
        jnp.zeros(tile_shape, jnp.float32),
        jnp.zeros(tile_shape, jnp.float32),
        jnp.zeros(tile_shape, jnp.float32),
        jnp.zeros((local_heads, rel_count), jnp.float32),
    )
    query_acc, key_acc, value_acc, bias_acc = lax.fori_loop(0, slot_top, second_pass, initial)
    query_part = from_tiles(logit_scale * query_acc).astype(jnp.bfloat16)
    key_terms = from_tiles(logit_scale * key_acc).astype(jnp.bfloat16)
    value_terms = from_tiles(value_acc).astype(jnp.bfloat16)
    return (query_part, key_terms, value_terms, bias_acc)


def per_device(
    saved_queries, saved_keys, saved_values, output_grad, rel_bias, key_tiles, live_count
):
    queries = saved_queries[0, 0]
    own_keys = saved_keys[0, 0]
    own_values = saved_values[0, 0]
    own_grad = output_grad[0, 0]
    tile_list = key_tiles[0]
    live_slots = live_count[0]
    tokens_here = own_keys.shape[0]
    group_size = HEADS // KVH
    wide_keys = jnp.repeat(own_keys.reshape(tokens_here, KVH, HD), group_size, axis=1).reshape(
        tokens_here, HEADS * HD
    )
    wide_values = jnp.repeat(own_values.reshape(tokens_here, KVH, HD), group_size, axis=1).reshape(
        tokens_here, HEADS * HD
    )
    head_grad, head_keys, head_values = (
        lax.all_to_all(own_grad, "seq", split_axis=1, concat_axis=0, tiled=True),
        lax.all_to_all(wide_keys, "seq", split_axis=1, concat_axis=0, tiled=True),
        lax.all_to_all(wide_values, "seq", split_axis=1, concat_axis=0, tiled=True),
    )
    slot_top = SLOTS
    query_part, key_terms, value_terms, bias_part = attention_grads(
        queries, head_keys, head_values, head_grad, rel_bias[0], tile_list, live_slots, slot_top
    )
    back_query, back_keys, back_values = (
        lax.all_to_all(query_part, "seq", split_axis=0, concat_axis=1, tiled=True),
        lax.all_to_all(key_terms, "seq", split_axis=0, concat_axis=1, tiled=True),
        lax.all_to_all(value_terms, "seq", split_axis=0, concat_axis=1, tiled=True),
    )
    key_grad = back_keys.reshape(tokens_here, KVH, group_size, HD).astype(jnp.float32).sum(2)
    key_grad = key_grad.reshape(tokens_here, KVH * HD).astype(jnp.bfloat16)
    value_grad = back_values.reshape(tokens_here, KVH, group_size, HD).astype(jnp.float32).sum(2)
    value_grad = value_grad.reshape(tokens_here, KVH * HD).astype(jnp.bfloat16)
    sent_query, sent_keys, sent_values = passed_along(
        (back_query, key_grad, value_grad), "pipe", -1
    )
    bias_share = lax.psum_scatter(bias_part, "dp", scatter_dimension=1, tiled=True)
    return (
        sent_query[None, None],
        sent_keys[None, None],
        sent_values[None, None],
        bias_share[None],
    )


def solution(mesh):
    placed = (
        P("pipe", "dp", None, "seq"),
        P("pipe", "dp", "seq", None),
        P("pipe", "dp", "seq", None),
        P("pipe", "dp", "seq", None),
        P("pipe", "seq", None),
        P("pipe", "seq", None, None),
        P("pipe", "seq", None),
    )
    return jax.shard_map(
        per_device,
        mesh=mesh,
        in_specs=placed,
        out_specs=(
            P("pipe", "dp", "seq", None),
            P("pipe", "dp", "seq", None),
            P("pipe", "dp", "seq", None),
            P("pipe", "seq", "dp"),
        ),
        check_vma=False,
    )
```

profile of v0, /device:TPU:6, one launch (start us, length us, event | category | flops | bytes accessed | tf_op | source)
XLA Modules:
  0.0 675.8 jit_solution(13860660114413350361)
XLA Ops:
  9.2 28.7 %all-to-all-start = ((bf16[128,32,64]{0,2,1:T(8,128)(2,1)}), bf16[128,32,64]{0,2,1:T(8,128)(2,1)S(1)}, u32[]{:S(2)}, u32[]{:S(2)}) async-start(bf16[128,32,64]{0,2,1:T(8,128)(2,1)} %bitcast.3), calls=%async_computation | async-start | bytes 1048576 | tf_op jit(solution)/shard_map/all_to_all | solution.py:186
  39.0 63.7 %all-to-all-done = bf16[128,32,64]{0,2,1:T(8,128)(2,1)S(1)} async-done(((bf16[128,32,64]{0,2,1:T(8,128)(2,1)}), bf16[128,32,64]{0,2,1:T(8,128)(2,1)S(1)}, u32[]{:S(2)}, u32[]{:S(2)}) %all-to-all-start) | async-done | bytes 524320 | tf_op jit(solution)/shard_map/all_to_all | solution.py:186
  103.7 3.9 all-to-all-start.1
  108.6 63.7 %all-to-all-done.1 = bf16[128,32,64]{0,2,1:T(8,128)(2,1)S(1)} async-done(((bf16[128,32,64]{0,2,1:T(8,128)(2,1)}), bf16[128,32,64]{0,2,1:T(8,128)(2,1)S(1)}, u32[]{:S(2)}, u32[]{:S(2)}) %all-to-all-start.1) | async-done | bytes 524320 | tf_op jit(solution)/shard_map/all_to_all | solution.py:187
  172.3 4.6 all-to-all-start.2
  180.0 61.3 %all-to-all-done.2 = bf16[128,32,64]{0,2,1:T(8,128)(2,1)} async-done(((bf16[128,32,64]{0,2,1:T(8,128)(2,1)}), bf16[128,32,64]{0,2,1:T(8,128)(2,1)}, u32[]{:S(2)}, u32[]{:S(2)}) %all-to-all-start.2) | async-done | bytes 524320 | tf_op jit(solution)/shard_map/all_to_all | solution.py:185
  241.3 61.3 %while.44 = (s32[]{:T(128)}, f32[1,32,128]{2,1,0:T(8,128)S(1)}, f32[1,32,128]{2,1,0:T(8,128)S(1)}, f32[1,32,128]{2,1,0:T(8,128)S(1)}, s32[1,32]{1,0:T(1,128)S(1)...) while((s32[]{:T(128)}, f32[1,32,128]{2,1,0:T(8,128)S(1)}, ...), condition=%wide.region_4.5_spmd.clone.clone, body=%wide.region_0.4_spmd.clone.clone.sunk | while | flops 247641984 | bytes 19312036 | solution.py:110
  302.6 137.4 %while.45 = (s32[]{:T(128)}, f32[1,32,128,64]{2,3,1,0:T(8,128)}, f32[1,32,128,64]{2,1,3,0:T(8,128)}, f32[1,32,128,64]{2,1,3,0:T(8,128)}, f32[1,256]{1,0:T(1,128)...) while((s32[]{:T(128)}, f32[1,32,128,64]{2,3,1,0:T(8,128)}, ...), condition=%wide.region_6.7_spmd.clone.clone, body=%wide.region_5.6_spmd.clone.clone.sunk | while | flops 751063424 | bytes 62607140 | solution.py:160
  309.4 4.3 fusion.157
  331.3 4.3 fusion.163
  342.6 4.3 fusion.157
  360.6 3.5 fusion.162
  366.0 4.3 fusion.163
  377.3 4.3 fusion.157
  400.7 4.3 fusion.163
  412.0 4.3 fusion.157
  435.4 4.3 fusion.163
  442.3 4.1 all-to-all-start.3
  447.9 61.2 %all-to-all-done.3 = bf16[32,128,64]{1,2,0:T(8,128)(2,1)S(1)} async-done(((bf16[32,128,64]{1,2,0:T(8,128)(2,1)}), bf16[32,128,64]{1,2,0:T(8,128)(2,1)S(1)}, u32[]{:S(2)}, u32[]{:S(2)}) %all-to-all-start.3) | async-done | bytes 524320 | tf_op jit(solution)/shard_map/all_to_all | solution.py:194
  509.1 3.9 all-to-all-start.4
  515.6 59.9 %all-to-all-done.4 = bf16[32,128,64]{1,2,0:T(8,128)(2,1)S(1)} async-done(((bf16[32,128,64]{1,2,0:T(8,128)(2,1)}), bf16[32,128,64]{1,2,0:T(8,128)(2,1)S(1)}, u32[]{:S(2)}, u32[]{:S(2)}) %all-to-all-start.4) | async-done | bytes 524320 | tf_op jit(solution)/shard_map/all_to_all | solution.py:195
  575.5 3.9 all-to-all-start.5
  582.1 59.8 %all-to-all-done.5 = bf16[32,128,64]{1,2,0:T(8,128)(2,1)S(1)} async-done(((bf16[32,128,64]{1,2,0:T(8,128)(2,1)}), bf16[32,128,64]{1,2,0:T(8,128)(2,1)S(1)}, u32[]{:S(2)}, u32[]{:S(2)}) %all-to-all-start.5) | async-done | bytes 524320 | tf_op jit(solution)/shard_map/all_to_all | solution.py:196
  644.1 20.9 %reduce-scatter.4.cloned.1.call-done = f32[64,1]{1,0:T(8,128)} async-done(((f32[256,1]{1,0:T(8,128)}), f32[64,1]{1,0:T(8,128)}) %reduce-scatter.4.cloned.1.call-update) | async-done | bytes 272
  (231 shorter events, 182.7 us)
Async XLA Ops:
  7.2 100.4 %copy-start.5 = (bf16[1,1,128,2048]{3,2,1,0:T(8,128)(2,1)S(1)}, bf16[1,1,128,2048]{3,2,1,0:T(8,128)(2,1)}, u32[]{:S(2)}) copy-start(bf16[1,1,128,2048]{3,2,1,0:T(8,128)(2,1)} %param.14) | copy-start | bytes 1572868
  9.2 93.6 %all-to-all-start = ((bf16[128,32,64]{0,2,1:T(8,128)(2,1)}), bf16[128,32,64]{0,2,1:T(8,128)(2,1)S(1)}, u32[]{:S(2)}, u32[]{:S(2)}) async-start(bf16[128,32,64]{0,2,1:T(8,128)(2,1)} %bitcast.3), calls=%async_computation | async-start | bytes 1048576 | tf_op jit(solution)/shard_map/all_to_all | solution.py:186
  37.9 139.0 %copy-start.6 = (bf16[1,1,4096,64]{2,3,1,0:T(8,128)(2,1)S(1)}, bf16[1,1,4096,64]{2,3,1,0:T(8,128)(2,1)}, u32[]{:S(2)}) copy-start(bf16[1,1,4096,64]{2,3,1,0:T(8,128)(2,1)} %param.11) | copy-start | bytes 1572868
  103.7 68.6 %all-to-all-start.1 = ((bf16[128,32,64]{0,2,1:T(8,128)(2,1)}), bf16[128,32,64]{0,2,1:T(8,128)(2,1)S(1)}, u32[]{:S(2)}, u32[]{:S(2)}) async-start(bf16[128,32,64]{0,2,1:T(8,128)(2,1)} %bitcast.9), calls=%async_computation.1 | async-start | bytes 1048576 | tf_op jit(solution)/shard_map/all_to_all | solution.py:187
  172.3 69.0 %all-to-all-start.2 = ((bf16[128,32,64]{0,2,1:T(8,128)(2,1)}), bf16[128,32,64]{0,2,1:T(8,128)(2,1)}, u32[]{:S(2)}, u32[]{:S(2)}) async-start(bf16[128,32,64]{0,2,1:T(8,128)(2,1)} %bitcast.12), calls=%async_computation.2 | async-start | bytes 1048576 | tf_op jit(solution)/shard_map/all_to_all | solution.py:185
  177.0 64.2 %copy-start.7 = (s32[1,1,32,4]{2,3,1,0:T(4,128)S(1)}, s32[1,1,32,4]{2,3,1,0:T(4,128)}, u32[]{:S(2)}) copy-start(s32[1,1,32,4]{2,3,1,0:T(4,128)} %param.16) | copy-start | bytes 1540
  177.1 64.2 %copy-start.8 = (f32[1,1,256]{2,1,0:T(1,128)S(1)}, f32[1,1,256]{2,1,0:T(1,128)}, u32[]{:S(2)}) copy-start(f32[1,1,256]{2,1,0:T(1,128)} %param.15) | copy-start | bytes 3076
  177.1 64.2 %copy-start.9 = (s32[1,1,32]{2,1,0:T(1,128)S(1)}, s32[1,1,32]{2,1,0:T(1,128)}, u32[]{:S(2)}) copy-start(s32[1,1,32]{2,1,0:T(1,128)} %param.17) | copy-start | bytes 388
  319.2 2.8 copy-start.1
  324.9 2.2 copy-start.3
  352.4 3.1 copy-start.1
  358.3 2.2 copy-start.3
  387.1 3.1 copy-start.1
  393.0 2.2 copy-start.3
  421.7 3.1 copy-start.1
  427.7 2.2 copy-start.3
  440.0 6.4 copy-start.4
  442.3 66.7 %all-to-all-start.3 = ((bf16[32,128,64]{1,2,0:T(8,128)(2,1)}), bf16[32,128,64]{1,2,0:T(8,128)(2,1)S(1)}, u32[]{:S(2)}, u32[]{:S(2)}) async-start(bf16[32,128,64]{1,2,0:T(8,128)(2,1)} %fusion.64), calls=%async_computation.3 | async-start | bytes 1048576 | tf_op jit(solution)/shard_map/all_to_all | solution.py:194
  509.1 66.4 %all-to-all-start.4 = ((bf16[32,128,64]{1,2,0:T(8,128)(2,1)}), bf16[32,128,64]{1,2,0:T(8,128)(2,1)S(1)}, u32[]{:S(2)}, u32[]{:S(2)}) async-start(bf16[32,128,64]{1,2,0:T(8,128)(2,1)} %fusion.65), calls=%async_computation.4 | async-start | bytes 1048576 | tf_op jit(solution)/shard_map/all_to_all | solution.py:195
  575.5 66.4 %all-to-all-start.5 = ((bf16[32,128,64]{1,2,0:T(8,128)(2,1)}), bf16[32,128,64]{1,2,0:T(8,128)(2,1)S(1)}, u32[]{:S(2)}, u32[]{:S(2)}) async-start(bf16[32,128,64]{1,2,0:T(8,128)(2,1)} %bitcast.204), calls=%async_computation.5 | async-start | bytes 1048576 | tf_op jit(solution)/shard_map/all_to_all | solution.py:196
  579.4 85.6 %reduce-scatter.4.cloned.1.call-start = ((), (), s32[]{:S(2)}) async-start(), calls=%async_computation.7 | async-start | bytes 163840
  579.4 88.5 %collective-permute-start = (bf16[128,2048]{0,1:T(8,128)(2,1)S(1)}, bf16[128,2048]{0,1:T(8,128)(2,1)S(1)}, u32[]{:S(2)}, u32[]{:S(2)}) collective-permute-start(bf16[128,2048]{0,1:T(8,128)(2,1)S(1)} %bitcast.313), channel_id=1, source_target_pairs={{4,0},{8,4},{12,8},{16,12},{20,16},{24,20},{28,24},{5,1},{9,5},{13... | collective-permute-start | bytes 1572872 | tf_op jit(solution)/shard_map/ppermute | solution.py:21
  580.8 85.5 %collective-permute-start.1 = (bf16[128,512]{0,1:T(8,128)(2,1)S(1)}, bf16[128,512]{0,1:T(8,128)(2,1)S(1)}, u32[]{:S(2)}, u32[]{:S(2)}) collective-permute-start(bf16[128,512]{0,1:T(8,128)(2,1)S(1)} %bitcast.319), channel_id=1, source_target_pairs={{4,0},{8,4},{12,8},{16,12},{20,16},{24,20},{28,24},{5,1},{9,5},{13... | collective-permute-start | bytes 393224 | tf_op jit(solution)/shard_map/ppermute | solution.py:21
  642.0 25.1 %collective-permute-start.2 = (bf16[128,512]{0,1:T(8,128)(2,1)S(1)}, bf16[128,512]{0,1:T(8,128)(2,1)S(1)}, u32[]{:S(2)}, u32[]{:S(2)}) collective-permute-start(bf16[128,512]{0,1:T(8,128)(2,1)S(1)} %bitcast.320), channel_id=1, source_target_pairs={{4,0},{8,4},{12,8},{16,12},{20,16},{24,20},{28,24},{5,1},{9,5},{13... | collective-permute-start | bytes 393224 | tf_op jit(solution)/shard_map/ppermute | solution.py:21
  (8 other events, 13.2 us)
Sparse Core Ops, SparseCore 0:
  644.2 20.7 reduce-scatter.3
where the time goes:
time: 678 us; the launch traced here: 676 us
  waiting for transfers between devices  390 us (58%)
  matrix products  133 us (20%)
  local copies, waits for them, and re-layouts  76.4 us (11%)
  starting transfers between devices  53 us (8%)
  between operations  14.3 us (2%)
  other arithmetic  8 us (1%)
    all_to_all x1, waiting for transfers between devices, per_device(): lax.all_to_all(wide_keys, 'seq', split_axis=1, concat_axis=0, tiled=True)  63.7 us
    all_to_all x1, waiting for transfers between devices, per_device(): lax.all_to_all(wide_values, 'seq', split_axis=1, concat_axis=0, tiled=True)  63.7 us
    all_to_all x1, waiting for transfers between devices, per_device(): lax.all_to_all(own_grad, 'seq', split_axis=1, concat_axis=0, tiled=True)  61.3 us
    all_to_all x1, waiting for transfers between devices, per_device(): lax.all_to_all(query_part, 'seq', split_axis=0, concat_axis=1, tiled=True)  61.2 us
    all_to_all x1, waiting for transfers between devices, per_device(): lax.all_to_all(key_terms, 'seq', split_axis=0, concat_axis=1, tiled=True)  59.9 us
    all_to_all x1, waiting for transfers between devices, per_device(): lax.all_to_all(value_terms, 'seq', split_axis=0, concat_axis=1, tiled=True)  59.8 us
    gather x24, local copies, waits for them, and re-layouts, attention_grads(): pick_tile = jax.vmap(lambda source, chosen: source[chosen])  36.9 us
    all_to_all x1, starting transfers between devices, per_device(): lax.all_to_all(wide_keys, 'seq', split_axis=1, concat_axis=0, tiled=True)  28.7 us
  transfers between devices with their start and end apart: 10, of which 7 were waited for; matrix products, arithmetic and copies ran while one was open for 2% of the time, Pallas kernels for 0%

commit v1 on v0

v1 whole, which is shorter than its diff:
```python
import jax
import jax.numpy as jnp
from jax import lax
from jax.experimental import pallas as pl
from jax.experimental.pallas import tpu as pltpu
from jax.sharding import PartitionSpec as P

HEADS = 32
KVH = 8
HD = 64
TILE = 128
BUCKET = 16
SLOTS = 4
GROUP = HEADS // KVH
QUART = TILE // GROUP
PACK = HD + QUART

neg_big = -1e30
log2_e = 1.4426950408889634
low = jnp.bfloat16
wide = jnp.float32

in_vmem = pl.BlockSpec(memory_space=pltpu.VMEM)
in_smem = pl.BlockSpec(memory_space=pltpu.SMEM)


def params(mib):
    return pltpu.CompilerParams(vmem_limit_bytes=mib << 20)


def pack_kernel(grad_ref, key_ref, value_ref, out_ref):
    for pair in range(HEADS // 2):
        turned = grad_ref[:, pair * 2 * HD : (pair + 1) * 2 * HD].T
        out_ref[2 * pair, 0:HD, :] = turned[0:HD]
        out_ref[2 * pair + 1, 0:HD, :] = turned[HD : 2 * HD]
    for g in range(KVH):
        both = jnp.concatenate(
            [key_ref[:, g * HD : (g + 1) * HD], value_ref[:, g * HD : (g + 1) * HD]], axis=1
        )
        for j in range(GROUP):
            out_ref[g * GROUP + j, HD:PACK, :] = both[j * QUART : (j + 1) * QUART]


def unpack_kernel(in_ref, query_ref, key_ref, value_ref):
    for pair in range(HEADS // 2):
        both = jnp.concatenate([in_ref[2 * pair, 0:HD, :], in_ref[2 * pair + 1, 0:HD, :]], axis=0)
        query_ref[:, pair * 2 * HD : (pair + 1) * 2 * HD] = both.T
    for pair in range(KVH // 2):
        sides = []
        for g in (2 * pair, 2 * pair + 1):
            sides.append(
                jnp.concatenate(
                    [in_ref[g * GROUP + j, HD:PACK, :] for j in range(GROUP)], axis=0
                )
            )
        at = slice(pair * 2 * HD, (pair + 1) * 2 * HD)
        key_ref[:, at] = jnp.concatenate([s[:, 0:HD] for s in sides], axis=1)
        value_ref[:, at] = jnp.concatenate([s[:, HD : 2 * HD] for s in sides], axis=1)


def sum_kernel(in_ref, out_ref):
    total = in_ref[0].astype(wide)
    for head in range(1, GROUP):
        total = total + in_ref[head].astype(wide)
    out_ref[...] = total.astype(low)


def table_kernel(steps_ref, table_ref):
    tiles_n = steps_ref.shape[0]
    for apart in range(tiles_n):
        near = steps_ref[apart : apart + 1, :]
        far = steps_ref[max(apart - 1, 0) : max(apart - 1, 0) + 1, :]
        line = jnp.broadcast_to(jnp.concatenate([near, far], axis=1) * log2_e, (TILE, 2 * TILE))
        turned = pltpu.roll(line, 0, 1, stride=1, stride_axis=0)[:, 0:TILE]
        if apart == 0:
            key_at = lax.broadcasted_iota(jnp.int32, (TILE, TILE), 0)
            query_at = lax.broadcasted_iota(jnp.int32, (TILE, TILE), 1)
            turned = jnp.where(key_at > query_at, neg_big, turned)
        table_ref[apart] = turned
    table_ref[tiles_n] = jnp.full((TILE, TILE), neg_big, wide)


def main_kernel(
    tiles_ref, live_ref, query_ref, recv_ref, kv_ref, table_ref,
    dq_ref, dkv_ref, steps_ref,
    kv, kt, acc, bias_acc,
):
    tiles_n = recv_ref.shape[0]
    scale = HD ** (-0.5)

    def begin(b, carry):
        both = jnp.concatenate([kv_ref[j, b] for j in range(GROUP)], axis=0)
        kv[b] = both
        kt[b] = both.T[0:HD]
        acc[b] = jnp.zeros((TILE, 2 * HD), wide)
        bias_acc[b] = jnp.zeros((TILE, TILE), wide)
        return carry

    lax.fori_loop(0, tiles_n, begin, 0)
    bias_acc[tiles_n] = jnp.zeros((TILE, TILE), wide)
    blank = jnp.zeros((HD, TILE), low)

    def one_tile(i, carry):
        live = live_ref[i]
        tile_at = [tiles_ref[i, s] for s in range(SLOTS)]
        apart = [jnp.where(s < live, i - tile_at[s], tiles_n) for s in range(SLOTS)]
        query = query_ref[:, pl.ds(pl.multiple_of(i * TILE, TILE), TILE)]
        weights = jnp.concatenate(
            [
                jnp.concatenate([query, blank], axis=1),
                jnp.concatenate([blank, recv_ref[i, 0:HD, :]], axis=1),
            ],
            axis=0,
        )
        keys = jnp.concatenate([kv[t] for t in tile_at], axis=0)
        both = jnp.dot(keys, weights, preferred_element_type=wide)
        bias = jnp.concatenate([table_ref[d] for d in apart], axis=0)
        logits = both[:, 0:TILE] * (scale * log2_e) + bias
        grad_prob = both[:, TILE : 2 * TILE]
        top = jnp.max(logits, axis=0, keepdims=True)
        raised = jnp.exp2(logits - top)
        probs = raised * (1.0 / jnp.sum(raised, axis=0, keepdims=True))
        delta = jnp.sum(probs * grad_prob, axis=0, keepdims=True)
        grad = probs * (grad_prob - delta)
        grad_low = grad.astype(low)
        terms = lax.dot_general(
            jnp.concatenate([grad_low, probs.astype(low)], axis=1),
            weights,
            (((1,), (1,)), ((), ())),
            preferred_element_type=wide,
        )
        keys_turned = jnp.concatenate([kt[t] for t in tile_at], axis=1)
        dq = jnp.dot(keys_turned, grad_low, preferred_element_type=wide)
        dq_ref[i] = (dq * scale).astype(low)
        for s in range(SLOTS):
            rows = slice(s * TILE, (s + 1) * TILE)
            acc[tile_at[s]] += terms[rows]
            bias_acc[apart[s]] += grad[rows]
        return carry

    lax.fori_loop(0, tiles_n, one_tile, 0)
    lane = lax.broadcasted_iota(jnp.int32, (TILE, 2 * HD), 1)
    sizes = jnp.where(lane < HD, scale, 1.0)
    blank_right = jnp.zeros((TILE, TILE), wide)
    in_bucket = lax.broadcasted_iota(jnp.int32, (BUCKET, 2 * TILE), 1) % BUCKET
    before = in_bucket < lax.broadcasted_iota(jnp.int32, (BUCKET, 2 * TILE), 0)

    def end(b, carry):
        terms = (acc[b] * sizes).astype(low)
        for j in range(GROUP):
            dkv_ref[j, b] = terms[j * QUART : (j + 1) * QUART]
        padded = jnp.concatenate([bias_acc[b], blank_right], axis=1)
        lined = padded[0:BUCKET]
        for step in range(1, TILE // BUCKET):
            rows = padded[step * BUCKET : (step + 1) * BUCKET]
            lined = lined + pltpu.roll(rows, 2 * TILE - step * BUCKET, 1)
        same = jnp.sum(jnp.where(before, 0.0, lined), axis=0, keepdims=True)
        less = jnp.sum(jnp.where(before, lined, 0.0), axis=0, keepdims=True)
        steps_ref[b] = same + pltpu.roll(less, 2 * TILE - BUCKET, 1)
        return carry

    lax.fori_loop(0, tiles_n, end, 0)


def make_table(bias_row, tiles_n):
    steps = jnp.repeat(bias_row.reshape(tiles_n, TILE // BUCKET), BUCKET, axis=1)
    return pl.pallas_call(
        table_kernel,
        out_shape=jax.ShapeDtypeStruct((tiles_n + 1, TILE, TILE), wide),
        in_specs=[in_vmem],
        out_specs=in_vmem,
        compiler_params=params(16),
    )(steps)


def head_grads(tile_list, live_slots, query, recv, kv_parts, table):
    tiles_n = recv.shape[0]
    return pl.pallas_call(
        main_kernel,
        out_shape=(
            jax.ShapeDtypeStruct((tiles_n, HD, TILE), low),
            jax.ShapeDtypeStruct((GROUP, tiles_n, QUART, 2 * HD), low),
            jax.ShapeDtypeStruct((tiles_n, 1, 2 * TILE), wide),
        ),
        in_specs=[in_smem, in_smem, in_vmem, in_vmem, in_vmem, in_vmem],
        out_specs=(in_vmem, in_vmem, in_vmem),
        scratch_shapes=[
            pltpu.VMEM((tiles_n, TILE, 2 * HD), low),
            pltpu.VMEM((tiles_n, HD, TILE), low),
            pltpu.VMEM((tiles_n, TILE, 2 * HD), wide),
            pltpu.VMEM((tiles_n + 1, TILE, TILE), wide),
        ],
        compiler_params=params(32),
    )(tile_list, live_slots, query, recv, kv_parts, table)


def bias_row_of(steps):
    near, far = steps[:, 0, 0:TILE], steps[:, 0, TILE : 2 * TILE]
    far = jnp.concatenate([far[1:], jnp.zeros_like(far[:1])], axis=0)
    tiles_n = steps.shape[0]
    return (near + far).reshape(1, tiles_n * (TILE // BUCKET), BUCKET).sum(2)


def per_device(
    saved_queries, saved_keys, saved_values, output_grad, rel_bias, key_tiles, live_count
):
    seq_n = lax.axis_size("seq")
    groups = [[g * GROUP + j for j in range(GROUP)] for g in range(seq_n // GROUP)]
    tiles_n = key_tiles.shape[2]
    packed = pl.pallas_call(
        pack_kernel,
        out_shape=jax.ShapeDtypeStruct((HEADS, PACK, TILE), low),
        in_specs=[in_vmem] * 3,
        out_specs=in_vmem,
        compiler_params=params(16),
    )(output_grad[0, 0], saved_keys[0, 0], saved_values[0, 0])
    recv = lax.all_to_all(packed, "seq", split_axis=0, concat_axis=0, tiled=True)
    kv_parts = lax.all_gather(recv[:, HD:PACK, :], "seq", axis=0, axis_index_groups=groups)
    table = make_table(rel_bias[0, 0], tiles_n)
    dq, dkv, steps = head_grads(
        key_tiles[0, 0], live_count[0, 0], saved_queries[0, 0].T, recv, kv_parts, table
    )
    bias_share = lax.psum_scatter(bias_row_of(steps), "dp", scatter_dimension=1, tiled=True)
    sections = lax.axis_size("pipe")
    back = [(p + 1, p) for p in range(sections - 1)]
    dq = lax.ppermute(dq, "pipe", back)
    terms = lax.all_to_all(
        dkv, "seq", split_axis=0, concat_axis=0, tiled=True, axis_index_groups=groups
    )
    summed = pl.pallas_call(
        sum_kernel,
        out_shape=jax.ShapeDtypeStruct((tiles_n, QUART, 2 * HD), low),
        in_specs=[in_vmem],
        out_specs=in_vmem,
        compiler_params=params(16),
    )(terms)
    summed = lax.ppermute(summed, "pipe", back)
    back_in = lax.all_to_all(
        jnp.concatenate([dq, summed], axis=1), "seq", split_axis=0, concat_axis=0, tiled=True
    )
    sent_query, sent_keys, sent_values = pl.pallas_call(
        unpack_kernel,
        out_shape=(
            jax.ShapeDtypeStruct((TILE, HEADS * HD), low),
            jax.ShapeDtypeStruct((TILE, KVH * HD), low),
            jax.ShapeDtypeStruct((TILE, KVH * HD), low),
        ),
        in_specs=[in_vmem],
        out_specs=(in_vmem,) * 3,
        compiler_params=params(16),
    )(back_in)
    return (
        sent_query[None, None],
        sent_keys[None, None],
        sent_values[None, None],
        bias_share[None],
    )


def solution(mesh):
    placed = (
        P("pipe", "dp", None, "seq"),
        P("pipe", "dp", "seq", None),
        P("pipe", "dp", "seq", None),
        P("pipe", "dp", "seq", None),
        P("pipe", "seq", None),
        P("pipe", "seq", None, None),
        P("pipe", "seq", None),
    )
    return jax.shard_map(
        per_device,
        mesh=mesh,
        in_specs=placed,
        out_specs=(
            P("pipe", "dp", "seq", None),
            P("pipe", "dp", "seq", None),
            P("pipe", "dp", "seq", None),
            P("pipe", "seq", "dp"),
        ),
        check_vma=False,
    )
```

time: 678 us -> 347 us (0.51)
  waiting for transfers between devices: 390 us -> 140 us
  matrix products: 133 us -> 0 us
  blocking collectives: 0 us -> 115 us
  local copies, waits for them, and re-layouts: 76.4 us -> 9.67 us
  Pallas kernels: 0 us -> 34.7 us
  starting transfers between devices: 53 us -> 27.7 us
    all_to_all x6 -> x2, waiting for transfers between devices: 370 us -> 64.4 us  [the longest x1 40 us: per_device(): lax.all_to_all(jnp.concatenate([dq, summed], axis=1), 'seq', split_axis=0...]
    dot_general x60 -> x0, matrix products: 133 us -> none  [the longest x8 28.5 us: slot_view(): jnp.einsum('hiad,hibd->hiab', query_blocks, current_key_block, preferred_...]
    all_to_all x0 -> x1, blocking collectives: none -> 115 us  [per_device(): lax.all_to_all(packed, 'seq', split_axis=0, concat_axis=0, tiled=True)]
    gather x24 -> x0, local copies, waits for them, and re-layouts: 36.9 us -> none  [attention_grads(): pick_tile = jax.vmap(lambda source, chosen: source[chosen])]
    pallas_call x0 -> x5, Pallas kernels: none -> 34.7 us  [the longest x1 32.1 us: head_grads(): pl.pallas_call(main_kernel, out_shape=(jax.ShapeDtypeStruct((tiles_n, HD,...]
    all_gather x0 -> x1, waiting for transfers between devices: none -> 28.2 us  [per_device(): lax.all_gather(recv[:, HD:PACK, :], 'seq', axis=0, axis_index_groups=groups)]
    unnamed x2 -> x3, waiting for transfers between devices: 20.9 us -> 45.6 us
    all_to_all x6 -> x2, starting transfers between devices: 49.1 us -> 25 us  [the longest x1 21.4 us: per_device(): lax.all_to_all(jnp.concatenate([dq, summed], axis=1), 'seq', split_axis=0...]
  transfers between devices with their start and end apart: 10 -> 6, of which waited for: 7 -> 5; matrix products, arithmetic and copies ran while one was open for 2% -> 1% of each run, Pallas kernels for 0% -> 0%
where the time goes in v1:
time: 347 us; the launch traced here: 344 us
  waiting for transfers between devices  140 us (40%)
  blocking collectives  115 us (33%)
  Pallas kernels  34.7 us (10%)
  starting transfers between devices  27.7 us (8%)
  between operations  14.2 us (4%)
  local copies, waits for them, and re-layouts  9.67 us (3%)
    all_to_all x1, blocking collectives, per_device(): lax.all_to_all(packed, 'seq', split_axis=0, concat_axis=0, tiled=True)  115 us
    unnamed x3, waiting for transfers between devices  45.6 us
    all_to_all x1, waiting for transfers between devices, per_device(): lax.all_to_all(jnp.concatenate([dq, summed], axis=1), 'seq', split_axis=0...  40 us
    pallas_call x1, Pallas kernels, head_grads(): pl.pallas_call(main_kernel, out_shape=(jax.ShapeDtypeStruct((tiles_n, HD,...  32.1 us
    all_gather x1, waiting for transfers between devices, per_device(): lax.all_gather(recv[:, HD:PACK, :], 'seq', axis=0, axis_index_groups=groups)  28.2 us
    all_to_all x1, waiting for transfers between devices, per_device(): lax.all_to_all(dkv, 'seq', split_axis=0, concat_axis=0, tiled=True, axis_...  24.4 us
    all_to_all x1, starting transfers between devices, per_device(): lax.all_to_all(jnp.concatenate([dq, summed], axis=1), 'seq', split_axis=0...  21.4 us
    unnamed x26, local copies, waits for them, and re-layouts  8.54 us
  transfers between devices with their start and end apart: 6, of which 5 were waited for; matrix products, arithmetic and copies ran while one was open for 1% of the time, Pallas kernels for 0%

profile of v1, /device:TPU:6, one launch (start us, length us, event | category | flops | bytes accessed | tf_op | source)
XLA Modules:
  0.0 343.7 jit_solution(2579860348135390512)
XLA Ops:
  7.2 1.0 copy-done.2
  8.3 0.9 copy-done.4
  9.2 0.9 copy-done.5
  10.4 115.4 %all_to_all.15.recv_ref = bf16[32,96,128]{2,1,0:T(8,128)(2,1)S(1)} all-to-all(bf16[32,96,128]{2,1,0:T(8,128)(2,1)S(1)} %shard_map.102), channel_id=1, replica_groups=mesh['seq'=32,'pipe'=8,'dp'=4] {'seq'}, dimensions={0} | all-to-all | bytes 1572864 | tf_op jit(solution)/shard_map/all_to_all | solution.py:217
  125.8 0.7 slice.18
  127.1 0.7 reduce.4
  128.0 1.1 shard_map.103.table_ref
  129.2 28.2 %all-gather.3.cloned.1.call-done = bf16[128,32,128]{2,1,0:T(8,128)(2,1)} async-done(((bf16[32,32,128]{2,1,0:T(8,128)(2,1)}), bf16[128,32,128]{2,1,0:T(8,128)(2,1)}) %all-gather.3.cloned.1.call-update) | async-done | bytes 1048592 | tf_op jit(solution)/shard_map/all_gather | solution.py:218
  157.4 1.2 copy-done
  158.6 32.1 %shard_map.104 = (bf16[32,64,128]{2,1,0:T(8,128)(2,1)S(1)}, bf16[4,32,32,128]{3,2,1,0:T(8,128)(2,1)S(1)}, f32[32,1,256]{2,1,0:T(1,128)S(1)}) custom-call(s32[32,4]{1,0:T(8,128)S(1)} %copy.19.tiles_ref, s32[32]{0:T(128)S(1)} %bitcast.29, bf16[64,4096]{1,0:T(8,128)(2,1)S(1)} %bitcast.26, bf16[32,96,128]{2,1,0:T(8,128)(2,1)S(1)} %all_to_all.15.recv_ref, ...), custom_call_target="tpu_custom_call" | custom-call | tf_op jit(solution)/shard_map/pallas_call | solution.py:178
  190.7 1.0 copy-done.1
  191.7 0.8 copy-done.7
  192.5 3.6 %all-to-all-start.1 = ((bf16[4,32,32,128]{3,2,1,0:T(8,128)(2,1)}), bf16[4,32,32,128]{3,2,1,0:T(8,128)(2,1)S(1)}, u32[]{:S(2)}, u32[]{:S(2)}) async-start(bf16[4,32,32,128]{3,2,1,0:T(8,128)(2,1)} %copy-done.1), calls=%async_computation.1 | async-start | bytes 2097152 | tf_op jit(solution)/shard_map/all_to_all | solution.py:227
  196.1 1.3 collective-permute-start
  197.4 24.4 %all-to-all-done.1.in_ref = bf16[4,32,32,128]{3,2,1,0:T(8,128)(2,1)S(1)} async-done(((bf16[4,32,32,128]{3,2,1,0:T(8,128)(2,1)}), bf16[4,32,32,128]{3,2,1,0:T(8,128)(2,1)S(1)}, u32[]{:S(2)}, u32[]{:S(2)}) %all-to-all-start.1) | async-done | bytes 1048608 | tf_op jit(solution)/shard_map/all_to_all | solution.py:227
  221.9 1.3 collective-permute-start.1
  223.3 2.1 collective-permute-done.1
  225.4 1.0 pad_maximum_fusion
  226.3 21.4 %all-to-all-start.2 = ((bf16[32,96,128]{2,1,0:T(8,128)(2,1)}), bf16[32,96,128]{2,1,0:T(8,128)(2,1)S(1)}, u32[]{:S(2)}, u32[]{:S(2)}) async-start(bf16[32,96,128]{2,1,0:T(8,128)(2,1)} %pad_maximum_fusion), calls=%async_computation.2 | async-start | bytes 1572864 | tf_op jit(solution)/shard_map/all_to_all | solution.py:238
  248.0 0.8 copy.21
  248.9 45.5 %reduce-scatter.4.cloned.1.call-done = f32[64,1]{1,0:T(8,128)} async-done(((f32[256,1]{1,0:T(8,128)}), f32[64,1]{1,0:T(8,128)}) %reduce-scatter.4.cloned.1.call-update) | async-done | bytes 272
  294.4 1.3 copy.22
  295.8 40.0 %all-to-all-done.2.in_ref = bf16[32,96,128]{2,1,0:T(8,128)(2,1)S(1)} async-done(((bf16[32,96,128]{2,1,0:T(8,128)(2,1)}), bf16[32,96,128]{2,1,0:T(8,128)(2,1)S(1)}, u32[]{:S(2)}, u32[]{:S(2)}) %all-to-all-start.2) | async-done | bytes 786464 | tf_op jit(solution)/shard_map/all_to_all | solution.py:238
  335.8 1.1 shard_map.106
  (35 shorter events, 1.6 us)
Async XLA Ops:
  7.2 150.2 %all-gather.3.cloned.1.call-start = ((), (), s32[]{:S(2)}) async-start(), calls=%async_computation.4 | async-start | bytes 1310720 | tf_op jit(solution)/shard_map/all_gather | solution.py:218
  7.2 1.0 copy-start.2
  8.3 0.9 copy-start.4
  9.2 0.9 copy-start.5
  10.3 116.7 %copy-start.10 = (f32[1,1,256]{2,1,0:T(1,128)S(1)}, f32[1,1,256]{2,1,0:T(1,128)}, u32[]{:S(2)}) copy-start(f32[1,1,256]{2,1,0:T(1,128)} %param.11) | copy-start | bytes 3076
  10.4 117.5 %copy-start.9 = (s32[1,1,32,4]{2,3,1,0:T(4,128)S(1)}, s32[1,1,32,4]{2,3,1,0:T(4,128)}, u32[]{:S(2)}) copy-start(s32[1,1,32,4]{2,3,1,0:T(4,128)} %param.12) | copy-start | bytes 1540
  125.8 31.6 %copy-start.3 = (bf16[1,1,4096,64]{2,3,1,0:T(8,128)(2,1)S(1)}, bf16[1,1,4096,64]{2,3,1,0:T(8,128)(2,1)}, u32[]{:S(2)}) copy-start(bf16[1,1,4096,64]{2,3,1,0:T(8,128)(2,1)} %param.7) | copy-start | bytes 1572868
  125.8 31.6 %copy-start.6 = (s32[1,1,32]{2,1,0:T(1,128)S(1)}, s32[1,1,32]{2,1,0:T(1,128)}, u32[]{:S(2)}) copy-start(s32[1,1,32]{2,1,0:T(1,128)} %param.13) | copy-start | bytes 388
  157.4 1.2 copy-start
  190.7 1.0 copy-start.1
  191.7 0.8 copy-start.7
  192.5 3.7 %copy-start.8 = (bf16[32,64,128]{2,1,0:T(8,128)(2,1)S(1)}, bf16[32,64,128]{2,1,0:T(8,128)(2,1)}, u32[]{:S(2)}) copy-start(bf16[32,64,128]{2,1,0:T(8,128)(2,1)} %copy-done.7) | copy-start | bytes 1572868
  192.5 29.3 %all-to-all-start.1 = ((bf16[4,32,32,128]{3,2,1,0:T(8,128)(2,1)}), bf16[4,32,32,128]{3,2,1,0:T(8,128)(2,1)S(1)}, u32[]{:S(2)}, u32[]{:S(2)}) async-start(bf16[4,32,32,128]{3,2,1,0:T(8,128)(2,1)} %copy-done.1), calls=%async_computation.1 | async-start | bytes 2097152 | tf_op jit(solution)/shard_map/all_to_all | solution.py:227
  196.1 27.1 %collective-permute-start = (bf16[32,64,128]{2,1,0:T(8,128)(2,1)S(1)}, bf16[32,64,128]{2,1,0:T(8,128)(2,1)S(1)}, u32[]{:S(2)}, u32[]{:S(2)}) collective-permute-start(bf16[32,64,128]{2,1,0:T(8,128)(2,1)S(1)} %copy-done.8), channel_id=1, source_target_pairs={{4,0},{8,4},{12,8},{16,12},{20,16},{24,20},{28,24},{5,1},{9,5},{13... | collective-permute-start | bytes 1572872 | tf_op jit(solution)/shard_map/ppermute | solution.py:226
  221.9 3.4 collective-permute-start.1
  226.3 109.4 %all-to-all-start.2 = ((bf16[32,96,128]{2,1,0:T(8,128)(2,1)}), bf16[32,96,128]{2,1,0:T(8,128)(2,1)S(1)}, u32[]{:S(2)}, u32[]{:S(2)}) async-start(bf16[32,96,128]{2,1,0:T(8,128)(2,1)} %pad_maximum_fusion), calls=%async_computation.2 | async-start | bytes 1572864 | tf_op jit(solution)/shard_map/all_to_all | solution.py:238
  247.7 46.7 %reduce-scatter.4.cloned.1.call-start = ((), (), s32[]{:S(2)}) async-start(), calls=%async_computation.5 | async-start | bytes 163840
Sparse Core Ops, SparseCore 0:
  126.7 30.6 all-gather.2
  252.5 41.8 reduce-scatter.3

commit v2 on v1

--- a/solution.py
+++ b/solution.py
@@ -28,11 +28,22 @@
     return pltpu.CompilerParams(vmem_limit_bytes=mib << 20)
 
 
-def pack_kernel(grad_ref, key_ref, value_ref, out_ref):
+def pack_kernel(grad_hbm, key_hbm, value_hbm, out_ref, grad_ref, key_ref, value_ref, sems):
+    copies = [
+        pltpu.make_async_copy(source, held, sems.at[n])
+        for n, (source, held) in enumerate(
+            ((grad_hbm, grad_ref), (key_hbm, key_ref), (value_hbm, value_ref))
+        )
+    ]
+    for copy in copies:
+        copy.start()
+    copies[0].wait()
     for pair in range(HEADS // 2):
         turned = grad_ref[:, pair * 2 * HD : (pair + 1) * 2 * HD].T
         out_ref[2 * pair, 0:HD, :] = turned[0:HD]
         out_ref[2 * pair + 1, 0:HD, :] = turned[HD : 2 * HD]
+    copies[1].wait()
+    copies[2].wait()
     for g in range(KVH):
         both = jnp.concatenate(
             [key_ref[:, g * HD : (g + 1) * HD], value_ref[:, g * HD : (g + 1) * HD]], axis=1
@@ -58,11 +69,13 @@
         value_ref[:, at] = jnp.concatenate([s[:, HD : 2 * HD] for s in sides], axis=1)
 
 
-def sum_kernel(in_ref, out_ref):
-    total = in_ref[0].astype(wide)
-    for head in range(1, GROUP):
-        total = total + in_ref[head].astype(wide)
-    out_ref[...] = total.astype(low)
+def sum_kernel(query_ref, *refs):
+    terms, out_ref = refs[:GROUP], refs[GROUP]
+    out_ref[:, 0:HD, :] = query_ref[...]
+    total = terms[0][...].astype(wide)
+    for term in terms[1:]:
+        total = total + term[...].astype(wide)
+    out_ref[:, HD:PACK, :] = total.astype(low)
 
 
 def table_kernel(steps_ref, table_ref):
@@ -81,74 +94,103 @@
 
 
 def main_kernel(
-    tiles_ref, live_ref, query_ref, recv_ref, kv_ref, table_ref,
-    dq_ref, dkv_ref, steps_ref,
-    kv, kt, acc, bias_acc,
+    place_ref, tiles_ref, live_ref, query_ref, recv_ref, *refs,
 ):
+    parts, table_ref, dq_ref = refs[: GROUP - 1], refs[GROUP - 1], refs[GROUP]
+    outs, steps_ref = refs[GROUP + 1 : 2 * GROUP + 1], refs[2 * GROUP + 1]
+    kv, kt, acc, bias_acc, even, odd = refs[2 * GROUP + 2 :]
     tiles_n = recv_ref.shape[0]
     scale = HD ** (-0.5)
+    place = place_ref[0]
+
+    def quarter(j):
+        return pl.ds(pl.multiple_of(lax.rem(j, GROUP) * QUART, QUART), QUART)
 
     def begin(b, carry):
-        both = jnp.concatenate([kv_ref[j, b] for j in range(GROUP)], axis=0)
-        kv[b] = both
-        kt[b] = both.T[0:HD]
-        acc[b] = jnp.zeros((TILE, 2 * HD), wide)
+        kv[b, quarter(place), :] = recv_ref[b, HD:PACK, :]
+        for d in range(1, GROUP):
+            kv[b, quarter(place + GROUP - d), :] = parts[d - 1][b]
+        kt[b] = kv[b].T[0:HD]
         bias_acc[b] = jnp.zeros((TILE, TILE), wide)
         return carry
 
-    lax.fori_loop(0, tiles_n, begin, 0)
+    lax.fori_loop(0, tiles_n, begin, 0, unroll=8)
     bias_acc[tiles_n] = jnp.zeros((TILE, TILE), wide)
     blank = jnp.zeros((HD, TILE), low)
-
-    def one_tile(i, carry):
-        live = live_ref[i]
-        tile_at = [tiles_ref[i, s] for s in range(SLOTS)]
-        apart = [jnp.where(s < live, i - tile_at[s], tiles_n) for s in range(SLOTS)]
+    slots = [slice(s * TILE, (s + 1) * TILE) for s in range(SLOTS)]
+
+    def weights_of(i):
         query = query_ref[:, pl.ds(pl.multiple_of(i * TILE, TILE), TILE)]
-        weights = jnp.concatenate(
+        return jnp.concatenate(
             [
                 jnp.concatenate([query, blank], axis=1),
                 jnp.concatenate([blank, recv_ref[i, 0:HD, :]], axis=1),
             ],
             axis=0,
         )
-        keys = jnp.concatenate([kv[t] for t in tile_at], axis=0)
-        both = jnp.dot(keys, weights, preferred_element_type=wide)
-        bias = jnp.concatenate([table_ref[d] for d in apart], axis=0)
-        logits = both[:, 0:TILE] * (scale * log2_e) + bias
-        grad_prob = both[:, TILE : 2 * TILE]
-        top = jnp.max(logits, axis=0, keepdims=True)
-        raised = jnp.exp2(logits - top)
-        probs = raised * (1.0 / jnp.sum(raised, axis=0, keepdims=True))
-        delta = jnp.sum(probs * grad_prob, axis=0, keepdims=True)
-        grad = probs * (grad_prob - delta)
-        grad_low = grad.astype(low)
+
+    def products(i):
+        keys = jnp.concatenate([kv[tiles_ref[i, s]] for s in range(SLOTS)], axis=0)
+        return jnp.dot(keys, weights_of(i), preferred_element_type=wide)
+
+    def rest(i, both):
+        live = live_ref[i]
+        tile_at = [tiles_ref[i, s] for s in range(SLOTS)]
+        apart = [jnp.where(s < live, i - tile_at[s], tiles_n) for s in range(SLOTS)]
+        logits = [
+            both[rows, 0:TILE] * (scale * log2_e) + table_ref[d] for rows, d in zip(slots, apart)
+        ]
+        most = jnp.maximum(jnp.maximum(logits[0], logits[1]), jnp.maximum(logits[2], logits[3]))
+        top = jnp.max(most, axis=0, keepdims=True)
+        raised, total, weighed = [], 0.0, 0.0
+        for rows, logit in zip(slots, logits):
+            raised.append(jnp.exp2(logit - top))
+            total = total + raised[-1]
+            weighed = weighed + raised[-1] * both[rows, TILE : 2 * TILE]
+        inverse = 1.0 / jnp.sum(total, axis=0, keepdims=True)
+        delta = jnp.sum(weighed, axis=0, keepdims=True) * inverse
+        probs_low, grad_low = [], []
+        for s in range(SLOTS):
+            probs = raised[s] * inverse
+            grad = probs * (both[slots[s], TILE : 2 * TILE] - delta)
+            bias_acc[apart[s]] += grad
+            probs_low.append(probs.astype(low))
+            grad_low.append(grad.astype(low))
+        grad_low = jnp.concatenate(grad_low, axis=0)
+        probs_low = jnp.concatenate(probs_low, axis=0)
         terms = lax.dot_general(
-            jnp.concatenate([grad_low, probs.astype(low)], axis=1),
-            weights,
+            jnp.concatenate([grad_low, probs_low], axis=1),
+            weights_of(i),
             (((1,), (1,)), ((), ())),
             preferred_element_type=wide,
         )
         keys_turned = jnp.concatenate([kt[t] for t in tile_at], axis=1)
         dq = jnp.dot(keys_turned, grad_low, preferred_element_type=wide)
         dq_ref[i] = (dq * scale).astype(low)
-        for s in range(SLOTS):
-            rows = slice(s * TILE, (s + 1) * TILE)
-            acc[tile_at[s]] += terms[rows]
-            bias_acc[apart[s]] += grad[rows]
+        acc[i] = terms[slots[0]]
+        for s in range(1, SLOTS):
+            acc[tile_at[s]] += terms[slots[s]]
+
+    even[...] = products(0)
+
+    def two_tiles(n, carry):
+        i = 2 * n
+        odd[...] = products(i + 1)
+        rest(i, even)
+        even[...] = products(jnp.minimum(i + 2, tiles_n - 1))
+        rest(i + 1, odd)
         return carry
 
-    lax.fori_loop(0, tiles_n, one_tile, 0)
-    lane = lax.broadcasted_iota(jnp.int32, (TILE, 2 * HD), 1)
+    lax.fori_loop(0, tiles_n // 2, two_tiles, 0, unroll=2)
+    lane = lax.broadcasted_iota(jnp.int32, (QUART, 2 * HD), 1)
     sizes = jnp.where(lane < HD, scale, 1.0)
     blank_right = jnp.zeros((TILE, TILE), wide)
     in_bucket = lax.broadcasted_iota(jnp.int32, (BUCKET, 2 * TILE), 1) % BUCKET
     before = in_bucket < lax.broadcasted_iota(jnp.int32, (BUCKET, 2 * TILE), 0)
 
     def end(b, carry):
-        terms = (acc[b] * sizes).astype(low)
-        for j in range(GROUP):
-            dkv_ref[j, b] = terms[j * QUART : (j + 1) * QUART]
+        for d in range(GROUP):
+            outs[d][b] = (acc[b, quarter(place + d), :] * sizes).astype(low)
         padded = jnp.concatenate([bias_acc[b], blank_right], axis=1)
         lined = padded[0:BUCKET]
         for step in range(1, TILE // BUCKET):
@@ -159,7 +201,7 @@
         steps_ref[b] = same + pltpu.roll(less, 2 * TILE - BUCKET, 1)
         return carry
 
-    lax.fori_loop(0, tiles_n, end, 0)
+    lax.fori_loop(0, tiles_n, end, 0, unroll=8)
 
 
 def make_table(bias_row, tiles_n):
@@ -173,25 +215,28 @@
     )(steps)
 
 
-def head_grads(tile_list, live_slots, query, recv, kv_parts, table):
+def head_grads(place, tile_list, live_slots, query, recv, parts, table):
     tiles_n = recv.shape[0]
+    share = jax.ShapeDtypeStruct((tiles_n, QUART, 2 * HD), low)
     return pl.pallas_call(
         main_kernel,
         out_shape=(
             jax.ShapeDtypeStruct((tiles_n, HD, TILE), low),
-            jax.ShapeDtypeStruct((GROUP, tiles_n, QUART, 2 * HD), low),
+            *[share] * GROUP,
             jax.ShapeDtypeStruct((tiles_n, 1, 2 * TILE), wide),
         ),
-        in_specs=[in_smem, in_smem, in_vmem, in_vmem, in_vmem, in_vmem],
-        out_specs=(in_vmem, in_vmem, in_vmem),
+        in_specs=[in_smem] * 3 + [in_vmem] * (GROUP + 2),
+        out_specs=(in_vmem,) * (GROUP + 2),
         scratch_shapes=[
             pltpu.VMEM((tiles_n, TILE, 2 * HD), low),
             pltpu.VMEM((tiles_n, HD, TILE), low),
             pltpu.VMEM((tiles_n, TILE, 2 * HD), wide),
             pltpu.VMEM((tiles_n + 1, TILE, TILE), wide),
+            pltpu.VMEM((SLOTS * TILE, 2 * TILE), wide),
+            pltpu.VMEM((SLOTS * TILE, 2 * TILE), wide),
         ],
         compiler_params=params(32),
-    )(tile_list, live_slots, query, recv, kv_parts, table)
+    )(place, tile_list, live_slots, query, recv, *parts, table)
 
 
 def bias_row_of(steps):
@@ -204,40 +249,57 @@
 def per_device(
     saved_queries, saved_keys, saved_values, output_grad, rel_bias, key_tiles, live_count
 ):
-    seq_n = lax.axis_size("seq")
-    groups = [[g * GROUP + j for j in range(GROUP)] for g in range(seq_n // GROUP)]
+    seq_n, sections = lax.axis_size("seq"), lax.axis_size("pipe")
     tiles_n = key_tiles.shape[2]
+
+    def passed_on(d):
+        return [
+            (g * GROUP + j, g * GROUP + (j + d) % GROUP)
+            for g in range(seq_n // GROUP)
+            for j in range(GROUP)
+        ]
+
     packed = pl.pallas_call(
         pack_kernel,
         out_shape=jax.ShapeDtypeStruct((HEADS, PACK, TILE), low),
-        in_specs=[in_vmem] * 3,
+        in_specs=[pl.BlockSpec(memory_space=pltpu.HBM)] * 3,
         out_specs=in_vmem,
+        scratch_shapes=[
+            pltpu.VMEM((TILE, HEADS * HD), low),
+            pltpu.VMEM((TILE, KVH * HD), low),
+            pltpu.VMEM((TILE, KVH * HD), low),
+            pltpu.SemaphoreType.DMA((3,)),
+        ],
         compiler_params=params(16),
     )(output_grad[0, 0], saved_keys[0, 0], saved_values[0, 0])
     recv = lax.all_to_all(packed, "seq", split_axis=0, concat_axis=0, tiled=True)
-    kv_parts = lax.all_gather(recv[:, HD:PACK, :], "seq", axis=0, axis_index_groups=groups)
     table = make_table(rel_bias[0, 0], tiles_n)
-    dq, dkv, steps = head_grads(
-        key_tiles[0, 0], live_count[0, 0], saved_queries[0, 0].T, recv, kv_parts, table
+    own, table = lax.optimization_barrier((recv[:, HD:PACK, :], table))
+    parts = [lax.ppermute(own, "seq", passed_on(d)) for d in range(1, GROUP)]
+    place = (lax.axis_index("seq") % GROUP).astype(jnp.int32).reshape(1)
+    dq, *terms, steps = head_grads(
+        place, key_tiles[0, 0], live_count[0, 0], saved_queries[0, 0].T, recv, parts, table
     )
     bias_share = lax.psum_scatter(bias_row_of(steps), "dp", scatter_dimension=1, tiled=True)
-    sections = lax.axis_size("pipe")
-    back = [(p + 1, p) for p in range(sections - 1)]
-    dq = lax.ppermute(dq, "pipe", back)
-    terms = lax.all_to_all(
-        dkv, "seq", split_axis=0, concat_axis=0, tiled=True, axis_index_groups=groups
-    )
-    summed = pl.pallas_call(
+
+    def moved(x, d):
+        pairs = [
+            (a * sections + p + 1, b * sections + p)
+            for a, b in passed_on(d)
+            for p in range(sections - 1)
+        ]
+        return lax.ppermute(x, ("seq", "pipe"), pairs)
+
+    terms = [moved(x, d) for d, x in enumerate(terms)]
+    dq = moved(dq, 0)
+    packed = pl.pallas_call(
         sum_kernel,
-        out_shape=jax.ShapeDtypeStruct((tiles_n, QUART, 2 * HD), low),
-        in_specs=[in_vmem],
+        out_shape=jax.ShapeDtypeStruct((tiles_n, PACK, TILE), low),
+        in_specs=[in_vmem] * (GROUP + 1),
         out_specs=in_vmem,
         compiler_params=params(16),
-    )(terms)
-    summed = lax.ppermute(summed, "pipe", back)
-    back_in = lax.all_to_all(
-        jnp.concatenate([dq, summed], axis=1), "seq", split_axis=0, concat_axis=0, tiled=True
-    )
+    )(dq, *terms)
+    back_in = lax.all_to_all(packed, "seq", split_axis=0, concat_axis=0, tiled=True)
     sent_query, sent_keys, sent_values = pl.pallas_call(
         unpack_kernel,
         out_shape=(

time: 347 us -> 302 us (0.87)
  the two profiles are of different devices: /device:TPU:6 before, /device:TPU:17 now
where the time goes in v2:
time: 302 us
  waiting for transfers between devices  198 us (66%)
  starting transfers between devices  63.9 us (21%)
  Pallas kernels  18 us (6%)
  between operations  14.3 us (5%)
  local copies, waits for them, and re-layouts  6.68 us (2%)
    all_to_all x2, waiting for transfers between devices, per_device(): lax.all_to_all(packed, 'seq', split_axis=0, concat_axis=0, tiled=True)  128 us
    unnamed x2, waiting for transfers between devices  40.1 us
    all_to_all x2, starting transfers between devices, per_device(): lax.all_to_all(packed, 'seq', split_axis=0, concat_axis=0, tiled=True)  40 us
    ppermute x3, waiting for transfers between devices, per_device(): parts = [lax.ppermute(own, 'seq', passed_on(d)) for d in range(1, GROUP)]  17.3 us
    ppermute x5, starting transfers between devices, moved(): return lax.ppermute(x, ('seq', 'pipe'), pairs)  16.6 us
    pallas_call x1, Pallas kernels, head_grads(): pl.pallas_call(main_kernel, out_shape=(jax.ShapeDtypeStruct((tiles_n, HD,...  13.1 us
    ppermute x5, waiting for transfers between devices, moved(): return lax.ppermute(x, ('seq', 'pipe'), pairs)  12.7 us
    ppermute x3, starting transfers between devices, per_device(): parts = [lax.ppermute(own, 'seq', passed_on(d)) for d in range(1, GROUP)]  7.2 us
  transfers between devices with their start and end apart: 11, of which 7 were waited for; matrix products, arithmetic and copies ran while one was open for 1% of the time, Pallas kernels for 0%

profile of v2, /device:TPU:17, one launch (start us, length us, event | category | flops | bytes accessed | tf_op | source)
XLA Modules:
  0.0 301.6 jit_solution(2915106219407071182)
XLA Ops:
  7.2 1.0 copy-done
  10.0 1.6 shard_map.102
  11.7 28.6 %all-to-all-start = ((bf16[32,96,128]{2,1,0:T(8,128)(2,1)}), bf16[32,96,128]{2,1,0:T(8,128)(2,1)S(1)}, u32[]{:S(2)}, u32[]{:S(2)}) async-start(bf16[32,96,128]{2,1,0:T(8,128)(2,1)} %shard_map.102), calls=%async_computation | async-start | bytes 1572864 | tf_op jit(solution)/shard_map/all_to_all | solution.py:275
  41.7 1.2 shard_map.103.refs_3_
  42.9 83.6 %all-to-all-done.recv_ref = bf16[32,96,128]{2,1,0:T(8,128)(2,1)S(1)} async-done(((bf16[32,96,128]{2,1,0:T(8,128)(2,1)}), bf16[32,96,128]{2,1,0:T(8,128)(2,1)S(1)}, u32[]{:S(2)}, u32[]{:S(2)}) %all-to-all-start) | async-done | bytes 786464 | tf_op jit(solution)/shard_map/all_to_all | solution.py:275
  127.2 1.9 collective-permute-start.2
  129.1 1.9 collective-permute-start.1
  131.0 3.4 %collective-permute-start = (bf16[32,32,128]{2,1,0:T(8,128)(2,1)}, bf16[32,32,128]{2,1,0:T(8,128)(2,1)}, u32[]{:S(2)}, u32[]{:S(2)}) collective-permute-start(bf16[32,32,128]{2,1,0:T(8,128)(2,1)} %slice.18), channel_id=1, source_target_pairs={{0,32},{32,64},{64,96},{96,0},{128,160},{160,192},{192,224},{224,1... | collective-permute-start | bytes 786440 | tf_op jit(solution)/shard_map/ppermute | solution.py:278
  134.5 1.4 collective-permute-done.2.refs_2_
  135.9 15.9 %collective-permute-done.1.refs_1_ = bf16[32,32,128]{2,1,0:T(8,128)(2,1)} collective-permute-done((bf16[32,32,128]{2,1,0:T(8,128)(2,1)}, bf16[32,32,128]{2,1,0:T(8,128)(2,1)}, u32[]{:S(2)}, u32[]{:S(2)}) %collective-permute-start.1) | collective-permute-done | bytes 262176 | tf_op jit(solution)/shard_map/ppermute | solution.py:278
  151.8 13.1 %shard_map.104 = (bf16[32,64,128]{2,1,0:T(8,128)(2,1)S(1)}, bf16[32,32,128]{2,1,0:T(8,128)(2,1)S(1)}, bf16[32,32,128]{2,1,0:T(8,128)(2,1)S(1)}, bf16[32,32,128]{...) custom-call(s32[1]{0:T(128)} %bitcast.2.place_ref, s32[32,4]{1,0:T(8,128)S(1)} %copy.19.tiles_ref, ...), custom_call_target="tpu_custom_call" | custom-call | tf_op jit(solution)/shard_map/pallas_call | solution.py:221
  164.9 3.0 collective-permute-start.3
  167.9 1.9 collective-permute-start.4
  169.8 3.4 %collective-permute-start.5 = (bf16[32,32,128]{2,1,0:T(8,128)(2,1)S(1)}, bf16[32,32,128]{2,1,0:T(8,128)(2,1)S(1)}, u32[]{:S(2)}, u32[]{:S(2)}) collective-permute-start(bf16[32,32,128]{2,1,0:T(8,128)(2,1)S(1)} %get-tuple-element.19), channel_id=1, source_target_pairs={{4,32},{8,36},{12,40},{16,44},{20,48},{24,52},{28,56},{36,64},{40,... | collective-permute-start | bytes 786440 | tf_op jit(solution)/shard_map/ppermute | solution.py:291
  173.3 3.8 %collective-permute-start.6 = (bf16[32,32,128]{2,1,0:T(8,128)(2,1)S(1)}, bf16[32,32,128]{2,1,0:T(8,128)(2,1)S(1)}, u32[]{:S(2)}, u32[]{:S(2)}) collective-permute-start(bf16[32,32,128]{2,1,0:T(8,128)(2,1)S(1)} %get-tuple-element.20), channel_id=1, source_target_pairs={{4,64},{8,68},{12,72},{16,76},{20,80},{24,84},{28,88},{36,96},{40,... | collective-permute-start | bytes 786440 | tf_op jit(solution)/shard_map/ppermute | solution.py:291
  177.1 4.4 %collective-permute-start.7 = (bf16[32,32,128]{2,1,0:T(8,128)(2,1)S(1)}, bf16[32,32,128]{2,1,0:T(8,128)(2,1)S(1)}, u32[]{:S(2)}, u32[]{:S(2)}) collective-permute-start(bf16[32,32,128]{2,1,0:T(8,128)(2,1)S(1)} %get-tuple-element.21), channel_id=1, source_target_pairs={{4,96},{8,100},{12,104},{16,108},{20,112},{24,116},{28,120},{36,0}... | collective-permute-start | bytes 786440 | tf_op jit(solution)/shard_map/ppermute | solution.py:291
  181.6 1.6 collective-permute-done.5.refs_1_
  183.2 11.1 %collective-permute-done.6.refs_2_ = bf16[32,32,128]{2,1,0:T(8,128)(2,1)S(1)} collective-permute-done((bf16[32,32,128]{2,1,0:T(8,128)(2,1)S(1)}, bf16[32,32,128]{2,1,0:T(8,128)(2,1)S(1)}, u32[]{:S(2)}, u32[]{:S(2)}) %collective-permute-start.6) | collective-permute-done | bytes 262176 | tf_op jit(solution)/shard_map/ppermute | solution.py:291
  194.3 1.1 shard_map.105
  195.4 11.4 %all-to-all-start.1 = ((bf16[32,96,128]{2,1,0:T(8,128)(2,1)}), bf16[32,96,128]{2,1,0:T(8,128)(2,1)S(1)}, u32[]{:S(2)}, u32[]{:S(2)}) async-start(bf16[32,96,128]{2,1,0:T(8,128)(2,1)} %shard_map.105), calls=%async_computation.1 | async-start | bytes 1572864 | tf_op jit(solution)/shard_map/all_to_all | solution.py:302
  208.0 40.0 %reduce-scatter.4.cloned.1.call-done = f32[64,1]{1,0:T(8,128)} async-done(((f32[256,1]{1,0:T(8,128)}), f32[64,1]{1,0:T(8,128)}) %reduce-scatter.4.cloned.1.call-update) | async-done | bytes 272
  248.0 1.3 copy.22
  249.3 44.4 %all-to-all-done.1.in_ref = bf16[32,96,128]{2,1,0:T(8,128)(2,1)S(1)} async-done(((bf16[32,96,128]{2,1,0:T(8,128)(2,1)}), bf16[32,96,128]{2,1,0:T(8,128)(2,1)S(1)}, u32[]{:S(2)}, u32[]{:S(2)}) %all-to-all-start.1) | async-done | bytes 786464 | tf_op jit(solution)/shard_map/all_to_all | solution.py:302
  293.7 1.1 shard_map.106
  (34 shorter events, 5.1 us)
Async XLA Ops:
  7.2 33.7 %copy-start.6 = (f32[1,1,256]{2,1,0:T(1,128)S(1)}, f32[1,1,256]{2,1,0:T(1,128)}, u32[]{:S(2)}) copy-start(f32[1,1,256]{2,1,0:T(1,128)} %param.11) | copy-start | bytes 3076
  7.2 1.0 copy-start
  8.2 0.9 copy-start.2
  9.1 0.9 copy-start.3
  11.7 122.7 %copy-start.5 = (s32[1,1,32,4]{2,3,1,0:T(4,128)S(1)}, s32[1,1,32,4]{2,3,1,0:T(4,128)}, u32[]{:S(2)}) copy-start(s32[1,1,32,4]{2,3,1,0:T(4,128)} %param.12) | copy-start | bytes 1540
  11.7 140.1 %copy-start.1 = (bf16[1,1,4096,64]{2,3,1,0:T(8,128)(2,1)S(1)}, bf16[1,1,4096,64]{2,3,1,0:T(8,128)(2,1)}, u32[]{:S(2)}) copy-start(bf16[1,1,4096,64]{2,3,1,0:T(8,128)(2,1)} %param.7) | copy-start | bytes 1572868
  11.7 140.1 %copy-start.4 = (s32[1,1,32]{2,1,0:T(1,128)S(1)}, s32[1,1,32]{2,1,0:T(1,128)}, u32[]{:S(2)}) copy-start(s32[1,1,32]{2,1,0:T(1,128)} %param.13) | copy-start | bytes 388
  11.7 114.7 %all-to-all-start = ((bf16[32,96,128]{2,1,0:T(8,128)(2,1)}), bf16[32,96,128]{2,1,0:T(8,128)(2,1)S(1)}, u32[]{:S(2)}, u32[]{:S(2)}) async-start(bf16[32,96,128]{2,1,0:T(8,128)(2,1)} %shard_map.102), calls=%async_computation | async-start | bytes 1572864 | tf_op jit(solution)/shard_map/all_to_all | solution.py:275
  127.2 8.8 %collective-permute-start.2 = (bf16[32,32,128]{2,1,0:T(8,128)(2,1)}, bf16[32,32,128]{2,1,0:T(8,128)(2,1)}, u32[]{:S(2)}, u32[]{:S(2)}) collective-permute-start(bf16[32,32,128]{2,1,0:T(8,128)(2,1)} %slice.18), channel_id=1, source_target_pairs={{0,96},{32,0},{64,32},{96,64},{128,224},{160,128},{192,160},{224,1... | collective-permute-start | bytes 786440 | tf_op jit(solution)/shard_map/ppermute | solution.py:278
  129.1 22.7 %collective-permute-start.1 = (bf16[32,32,128]{2,1,0:T(8,128)(2,1)}, bf16[32,32,128]{2,1,0:T(8,128)(2,1)}, u32[]{:S(2)}, u32[]{:S(2)}) collective-permute-start(bf16[32,32,128]{2,1,0:T(8,128)(2,1)} %slice.18), channel_id=1, source_target_pairs={{0,64},{32,96},{64,0},{96,32},{128,192},{160,224},{192,128},{224,1... | collective-permute-start | bytes 786440 | tf_op jit(solution)/shard_map/ppermute | solution.py:278
  131.0 20.8 %collective-permute-start = (bf16[32,32,128]{2,1,0:T(8,128)(2,1)}, bf16[32,32,128]{2,1,0:T(8,128)(2,1)}, u32[]{:S(2)}, u32[]{:S(2)}) collective-permute-start(bf16[32,32,128]{2,1,0:T(8,128)(2,1)} %slice.18), channel_id=1, source_target_pairs={{0,32},{32,64},{64,96},{96,0},{128,160},{160,192},{192,224},{224,1... | collective-permute-start | bytes 786440 | tf_op jit(solution)/shard_map/ppermute | solution.py:278
  164.9 29.4 %collective-permute-start.3 = (bf16[32,64,128]{2,1,0:T(8,128)(2,1)S(1)}, bf16[32,64,128]{2,1,0:T(8,128)(2,1)S(1)}, u32[]{:S(2)}, u32[]{:S(2)}) collective-permute-start(bf16[32,64,128]{2,1,0:T(8,128)(2,1)S(1)} %get-tuple-element.17), channel_id=1, source_target_pairs={{4,0},{8,4},{12,8},{16,12},{20,16},{24,20},{28,24},{36,32},{40,36}... | collective-permute-start | bytes 1572872 | tf_op jit(solution)/shard_map/ppermute | solution.py:291
  167.9 13.7 %collective-permute-start.4 = (bf16[32,32,128]{2,1,0:T(8,128)(2,1)S(1)}, bf16[32,32,128]{2,1,0:T(8,128)(2,1)S(1)}, u32[]{:S(2)}, u32[]{:S(2)}) collective-permute-start(bf16[32,32,128]{2,1,0:T(8,128)(2,1)S(1)} %get-tuple-element.18), channel_id=1, source_target_pairs={{4,0},{8,4},{12,8},{16,12},{20,16},{24,20},{28,24},{36,32},{40,36}... | collective-permute-start | bytes 786440 | tf_op jit(solution)/shard_map/ppermute | solution.py:291
  169.8 13.4 %collective-permute-start.5 = (bf16[32,32,128]{2,1,0:T(8,128)(2,1)S(1)}, bf16[32,32,128]{2,1,0:T(8,128)(2,1)S(1)}, u32[]{:S(2)}, u32[]{:S(2)}) collective-permute-start(bf16[32,32,128]{2,1,0:T(8,128)(2,1)S(1)} %get-tuple-element.19), channel_id=1, source_target_pairs={{4,32},{8,36},{12,40},{16,44},{20,48},{24,52},{28,56},{36,64},{40,... | collective-permute-start | bytes 786440 | tf_op jit(solution)/shard_map/ppermute | solution.py:291
  173.3 21.0 %collective-permute-start.6 = (bf16[32,32,128]{2,1,0:T(8,128)(2,1)S(1)}, bf16[32,32,128]{2,1,0:T(8,128)(2,1)S(1)}, u32[]{:S(2)}, u32[]{:S(2)}) collective-permute-start(bf16[32,32,128]{2,1,0:T(8,128)(2,1)S(1)} %get-tuple-element.20), channel_id=1, source_target_pairs={{4,64},{8,68},{12,72},{16,76},{20,80},{24,84},{28,88},{36,96},{40,... | collective-permute-start | bytes 786440 | tf_op jit(solution)/shard_map/ppermute | solution.py:291
  177.1 17.2 %collective-permute-start.7 = (bf16[32,32,128]{2,1,0:T(8,128)(2,1)S(1)}, bf16[32,32,128]{2,1,0:T(8,128)(2,1)S(1)}, u32[]{:S(2)}, u32[]{:S(2)}) collective-permute-start(bf16[32,32,128]{2,1,0:T(8,128)(2,1)S(1)} %get-tuple-element.21), channel_id=1, source_target_pairs={{4,96},{8,100},{12,104},{16,108},{20,112},{24,116},{28,120},{36,0}... | collective-permute-start | bytes 786440 | tf_op jit(solution)/shard_map/ppermute | solution.py:291
  195.4 98.4 %all-to-all-start.1 = ((bf16[32,96,128]{2,1,0:T(8,128)(2,1)}), bf16[32,96,128]{2,1,0:T(8,128)(2,1)S(1)}, u32[]{:S(2)}, u32[]{:S(2)}) async-start(bf16[32,96,128]{2,1,0:T(8,128)(2,1)} %shard_map.105), calls=%async_computation.1 | async-start | bytes 1572864 | tf_op jit(solution)/shard_map/all_to_all | solution.py:302
  206.8 41.2 %reduce-scatter.4.cloned.1.call-start = ((), (), s32[]{:S(2)}) async-start(), calls=%async_computation.3 | async-start | bytes 163840
Sparse Core Ops, SparseCore 0:
  211.6 36.3 reduce-scatter.3

commit v3 on v2

--- a/solution.py
+++ b/solution.py
@@ -69,11 +69,11 @@
         value_ref[:, at] = jnp.concatenate([s[:, HD : 2 * HD] for s in sides], axis=1)
 
 
-def sum_kernel(query_ref, *refs):
-    terms, out_ref = refs[:GROUP], refs[GROUP]
-    out_ref[:, 0:HD, :] = query_ref[...]
-    total = terms[0][...].astype(wide)
-    for term in terms[1:]:
+def sum_kernel(own_ref, *refs):
+    terms, out_ref = refs[:-1], refs[-1]
+    out_ref[:, 0:HD, :] = own_ref[:, 0:HD, :]
+    total = own_ref[:, HD:PACK, :].astype(wide)
+    for term in terms:
         total = total + term[...].astype(wide)
     out_ref[:, HD:PACK, :] = total.astype(low)
 
@@ -96,9 +96,9 @@
 def main_kernel(
     place_ref, tiles_ref, live_ref, query_ref, recv_ref, *refs,
 ):
-    parts, table_ref, dq_ref = refs[: GROUP - 1], refs[GROUP - 1], refs[GROUP]
-    outs, steps_ref = refs[GROUP + 1 : 2 * GROUP + 1], refs[2 * GROUP + 1]
-    kv, kt, acc, bias_acc, even, odd = refs[2 * GROUP + 2 :]
+    parts, table_ref, own_ref = refs[: GROUP - 1], refs[GROUP - 1], refs[GROUP]
+    outs, steps_ref = refs[GROUP + 1 : 2 * GROUP], refs[2 * GROUP]
+    kv, kt, acc, bias_acc, even, odd = refs[2 * GROUP + 1 :]
     tiles_n = recv_ref.shape[0]
     scale = HD ** (-0.5)
     place = place_ref[0]
@@ -166,7 +166,7 @@
         )
         keys_turned = jnp.concatenate([kt[t] for t in tile_at], axis=1)
         dq = jnp.dot(keys_turned, grad_low, preferred_element_type=wide)
-        dq_ref[i] = (dq * scale).astype(low)
+        own_ref[i, 0:HD, :] = (dq * scale).astype(low)
         acc[i] = terms[slots[0]]
         for s in range(1, SLOTS):
             acc[tile_at[s]] += terms[slots[s]]
@@ -181,7 +181,7 @@
         rest(i + 1, odd)
         return carry
 
-    lax.fori_loop(0, tiles_n // 2, two_tiles, 0, unroll=2)
+    lax.fori_loop(0, tiles_n // 2, two_tiles, 0, unroll=4)
     lane = lax.broadcasted_iota(jnp.int32, (QUART, 2 * HD), 1)
     sizes = jnp.where(lane < HD, scale, 1.0)
     blank_right = jnp.zeros((TILE, TILE), wide)
@@ -189,8 +189,9 @@
     before = in_bucket < lax.broadcasted_iota(jnp.int32, (BUCKET, 2 * TILE), 0)
 
     def end(b, carry):
-        for d in range(GROUP):
-            outs[d][b] = (acc[b, quarter(place + d), :] * sizes).astype(low)
+        own_ref[b, HD:PACK, :] = (acc[b, quarter(place), :] * sizes).astype(low)
+        for d in range(1, GROUP):
+            outs[d - 1][b] = (acc[b, quarter(place + d), :] * sizes).astype(low)
         padded = jnp.concatenate([bias_acc[b], blank_right], axis=1)
         lined = padded[0:BUCKET]
         for step in range(1, TILE // BUCKET):
@@ -221,12 +222,12 @@
     return pl.pallas_call(
         main_kernel,
         out_shape=(
-            jax.ShapeDtypeStruct((tiles_n, HD, TILE), low),
-            *[share] * GROUP,
+            jax.ShapeDtypeStruct((tiles_n, PACK, TILE), low),
+            *[share] * (GROUP - 1),
             jax.ShapeDtypeStruct((tiles_n, 1, 2 * TILE), wide),
         ),
         in_specs=[in_smem] * 3 + [in_vmem] * (GROUP + 2),
-        out_specs=(in_vmem,) * (GROUP + 2),
+        out_specs=(in_vmem,) * (GROUP + 1),
         scratch_shapes=[
             pltpu.VMEM((tiles_n, TILE, 2 * HD), low),
             pltpu.VMEM((tiles_n, HD, TILE), low),
@@ -258,6 +259,9 @@
             for g in range(seq_n // GROUP)
             for j in range(GROUP)
         ]
+
+    def held(x):
+        return pltpu.with_memory_space_constraint(x, pltpu.HBM)
 
     packed = pl.pallas_call(
         pack_kernel,
@@ -271,13 +275,13 @@
             pltpu.SemaphoreType.DMA((3,)),
         ],
         compiler_params=params(16),
-    )(output_grad[0, 0], saved_keys[0, 0], saved_values[0, 0])
+    )(*[held(x[0, 0]) for x in (output_grad, saved_keys, saved_values)])
     recv = lax.all_to_all(packed, "seq", split_axis=0, concat_axis=0, tiled=True)
     table = make_table(rel_bias[0, 0], tiles_n)
-    own, table = lax.optimization_barrier((recv[:, HD:PACK, :], table))
-    parts = [lax.ppermute(own, "seq", passed_on(d)) for d in range(1, GROUP)]
+    quarters, table = lax.optimization_barrier((recv[:, HD:PACK, :], table))
+    parts = [lax.ppermute(quarters, "seq", passed_on(d)) for d in range(1, GROUP)]
     place = (lax.axis_index("seq") % GROUP).astype(jnp.int32).reshape(1)
-    dq, *terms, steps = head_grads(
+    own, *terms, steps = head_grads(
         place, key_tiles[0, 0], live_count[0, 0], saved_queries[0, 0].T, recv, parts, table
     )
     bias_share = lax.psum_scatter(bias_row_of(steps), "dp", scatter_dimension=1, tiled=True)
@@ -290,15 +294,15 @@
         ]
         return lax.ppermute(x, ("seq", "pipe"), pairs)
 
-    terms = [moved(x, d) for d, x in enumerate(terms)]
-    dq = moved(dq, 0)
+    terms = [moved(x, d) for d, x in enumerate(terms, 1)]
+    own = moved(own, 0)
     packed = pl.pallas_call(
         sum_kernel,
         out_shape=jax.ShapeDtypeStruct((tiles_n, PACK, TILE), low),
-        in_specs=[in_vmem] * (GROUP + 1),
+        in_specs=[in_vmem] * GROUP,
         out_specs=in_vmem,
         compiler_params=params(16),
-    )(dq, *terms)
+    )(own, *terms)
     back_in = lax.all_to_all(packed, "seq", split_axis=0, concat_axis=0, tiled=True)
     sent_query, sent_keys, sent_values = pl.pallas_call(
         unpack_kernel,

time: 302 us -> 298 us (0.987)
  the two profiles are of different devices: /device:TPU:17 before, /device:TPU:15 now
where the time goes in v3:
time: 298 us
  waiting for transfers between devices  200 us (67%)
  starting transfers between devices  60.7 us (20%)
  Pallas kernels  17.9 us (6%)
  between operations  14.2 us (5%)
  local copies, waits for them, and re-layouts  3.83 us (1%)
    all_to_all x2, waiting for transfers between devices, per_device(): lax.all_to_all(packed, 'seq', split_axis=0, concat_axis=0, tiled=True)  131 us
    all_to_all x2, starting transfers between devices, per_device(): lax.all_to_all(packed, 'seq', split_axis=0, concat_axis=0, tiled=True)  40 us
    unnamed x2, waiting for transfers between devices  38.3 us
    ppermute x3, waiting for transfers between devices, per_device(): lax.ppermute(quarters, 'seq', passed_on(d))  17.3 us
    ppermute x4, starting transfers between devices, moved(): return lax.ppermute(x, ('seq', 'pipe'), pairs)  13.5 us
    ppermute x4, waiting for transfers between devices, moved(): return lax.ppermute(x, ('seq', 'pipe'), pairs)  13.4 us
    pallas_call x1, Pallas kernels, head_grads(): pl.pallas_call(main_kernel, out_shape=(jax.ShapeDtypeStruct((tiles_n, PAC...  12.4 us
    ppermute x3, starting transfers between devices, per_device(): lax.ppermute(quarters, 'seq', passed_on(d))  7.2 us
  transfers between devices with their start and end apart: 10, of which 7 were waited for; matrix products, arithmetic and copies ran while one was open for 1% of the time, Pallas kernels for 0%

profile of v3, /device:TPU:15, one launch (start us, length us, event | category | flops | bytes accessed | tf_op | source)
XLA Modules:
  0.0 297.5 jit_solution(6946266326739045256)
XLA Ops:
  7.2 2.3 shard_map.102
  9.5 28.6 %all-to-all-start = ((bf16[32,96,128]{2,1,0:T(8,128)(2,1)}), bf16[32,96,128]{2,1,0:T(8,128)(2,1)S(1)}, u32[]{:S(2)}, u32[]{:S(2)}) async-start(bf16[32,96,128]{2,1,0:T(8,128)(2,1)} %shard_map.102), calls=%async_computation | async-start | bytes 1572864 | tf_op jit(solution)/shard_map/all_to_all | solution.py:279
  39.5 1.2 shard_map.103.refs_3_
  40.7 83.6 %all-to-all-done.recv_ref = bf16[32,96,128]{2,1,0:T(8,128)(2,1)S(1)} async-done(((bf16[32,96,128]{2,1,0:T(8,128)(2,1)}), bf16[32,96,128]{2,1,0:T(8,128)(2,1)S(1)}, u32[]{:S(2)}, u32[]{:S(2)}) %all-to-all-start) | async-done | bytes 786464 | tf_op jit(solution)/shard_map/all_to_all | solution.py:279
  124.2 0.7 slice.18
  125.0 1.9 collective-permute-start.2
  126.9 1.9 collective-permute-start.1
  128.8 3.4 %collective-permute-start = (bf16[32,32,128]{2,1,0:T(8,128)(2,1)}, bf16[32,32,128]{2,1,0:T(8,128)(2,1)}, u32[]{:S(2)}, u32[]{:S(2)}) collective-permute-start(bf16[32,32,128]{2,1,0:T(8,128)(2,1)} %slice.18), channel_id=1, source_target_pairs={{0,32},{32,64},{64,96},{96,0},{128,160},{160,192},{192,224},{224,1... | collective-permute-start | bytes 786440 | tf_op jit(solution)/shard_map/ppermute | solution.py:282
  132.3 1.4 collective-permute-done.2.refs_2_
  133.7 15.9 %collective-permute-done.1.refs_1_ = bf16[32,32,128]{2,1,0:T(8,128)(2,1)} collective-permute-done((bf16[32,32,128]{2,1,0:T(8,128)(2,1)}, bf16[32,32,128]{2,1,0:T(8,128)(2,1)}, u32[]{:S(2)}, u32[]{:S(2)}) %collective-permute-start.1) | collective-permute-done | bytes 262176 | tf_op jit(solution)/shard_map/ppermute | solution.py:282
  149.6 12.4 %shard_map.104 = (bf16[32,96,128]{2,1,0:T(8,128)(2,1)S(1)}, bf16[32,32,128]{2,1,0:T(8,128)(2,1)S(1)}, bf16[32,32,128]{2,1,0:T(8,128)(2,1)S(1)}, bf16[32,32,128]{2,1,0:T(8,128)(2,1)S(1)}, f32[32,1,256]{2,1,0:T(1,128)S(1)}) custom-call(s32[1]{0:T(128)} %bitcast.2.place_ref, s32[32,4]{1,0:T(8,128)S(1)} %copy.19.tiles_ref, s32[32]{0:T(128)S(1)} %bitcast.25, ...), custom_call_target="tpu_custom_call" | custom-call | tf_op jit(solution)/shard_map/pallas_call | solution.py:222
  162.0 3.0 collective-permute-start.3
  165.0 2.9 collective-permute-start.4
  167.9 3.9 %collective-permute-start.5 = (bf16[32,32,128]{2,1,0:T(8,128)(2,1)S(1)}, bf16[32,32,128]{2,1,0:T(8,128)(2,1)S(1)}, u32[]{:S(2)}, u32[]{:S(2)}) collective-permute-start(bf16[32,32,128]{2,1,0:T(8,128)(2,1)S(1)} %get-tuple-element.18), channel_id=1, source_target_pairs={{4,64},{8,68},{12,72},{16,76},{20,80},{24,84},{28,88},{36,96},{40,... | collective-permute-start | bytes 786440 | tf_op jit(solution)/shard_map/ppermute | solution.py:295
  171.8 3.7 %collective-permute-start.6 = (bf16[32,32,128]{2,1,0:T(8,128)(2,1)S(1)}, bf16[32,32,128]{2,1,0:T(8,128)(2,1)S(1)}, u32[]{:S(2)}, u32[]{:S(2)}) collective-permute-start(bf16[32,32,128]{2,1,0:T(8,128)(2,1)S(1)} %get-tuple-element.19), channel_id=1, source_target_pairs={{4,96},{8,100},{12,104},{16,108},{20,112},{24,116},{28,120},{36,0}... | collective-permute-start | bytes 786440 | tf_op jit(solution)/shard_map/ppermute | solution.py:295
  175.5 2.7 collective-permute-done.4.refs_0_
  178.2 10.7 %collective-permute-done.5.refs_1_ = bf16[32,32,128]{2,1,0:T(8,128)(2,1)S(1)} collective-permute-done((bf16[32,32,128]{2,1,0:T(8,128)(2,1)S(1)}, bf16[32,32,128]{2,1,0:T(8,128)(2,1)S(1)}, u32[]{:S(2)}, u32[]{:S(2)}) %collective-permute-start.5) | collective-permute-done | bytes 262176 | tf_op jit(solution)/shard_map/ppermute | solution.py:295
  188.9 1.1 shard_map.105
  190.0 11.4 %all-to-all-start.1 = ((bf16[32,96,128]{2,1,0:T(8,128)(2,1)}), bf16[32,96,128]{2,1,0:T(8,128)(2,1)S(1)}, u32[]{:S(2)}, u32[]{:S(2)}) async-start(bf16[32,96,128]{2,1,0:T(8,128)(2,1)} %shard_map.105), calls=%async_computation.1 | async-start | bytes 1572864 | tf_op jit(solution)/shard_map/all_to_all | solution.py:306
  201.7 0.8 copy.21
  202.5 38.3 %reduce-scatter.4.cloned.1.call-done = f32[64,1]{1,0:T(8,128)} async-done(((f32[256,1]{1,0:T(8,128)}), f32[64,1]{1,0:T(8,128)}) %reduce-scatter.4.cloned.1.call-update) | async-done | bytes 272
  240.8 1.3 copy.22
  242.1 47.5 %all-to-all-done.1.in_ref = bf16[32,96,128]{2,1,0:T(8,128)(2,1)S(1)} async-done(((bf16[32,96,128]{2,1,0:T(8,128)(2,1)}), bf16[32,96,128]{2,1,0:T(8,128)(2,1)S(1)}, u32[]{:S(2)}, u32[]{:S(2)}) %all-to-all-start.1) | async-done | bytes 786464 | tf_op jit(solution)/shard_map/all_to_all | solution.py:306
  289.6 1.1 shard_map.106
  (26 shorter events, 1.8 us)
Async XLA Ops:
  7.2 31.5 %copy-start.3 = (f32[1,1,256]{2,1,0:T(1,128)S(1)}, f32[1,1,256]{2,1,0:T(1,128)}, u32[]{:S(2)}) copy-start(f32[1,1,256]{2,1,0:T(1,128)} %param.11) | copy-start | bytes 3076
  9.5 122.7 %copy-start.2 = (s32[1,1,32,4]{2,3,1,0:T(4,128)S(1)}, s32[1,1,32,4]{2,3,1,0:T(4,128)}, u32[]{:S(2)}) copy-start(s32[1,1,32,4]{2,3,1,0:T(4,128)} %param.12) | copy-start | bytes 1540
  9.5 140.1 %copy-start = (bf16[1,1,4096,64]{2,3,1,0:T(8,128)(2,1)S(1)}, bf16[1,1,4096,64]{2,3,1,0:T(8,128)(2,1)}, u32[]{:S(2)}) copy-start(bf16[1,1,4096,64]{2,3,1,0:T(8,128)(2,1)} %param.7) | copy-start | bytes 1572868
  9.5 140.1 %copy-start.1 = (s32[1,1,32]{2,1,0:T(1,128)S(1)}, s32[1,1,32]{2,1,0:T(1,128)}, u32[]{:S(2)}) copy-start(s32[1,1,32]{2,1,0:T(1,128)} %param.13) | copy-start | bytes 388
  9.5 114.7 %all-to-all-start = ((bf16[32,96,128]{2,1,0:T(8,128)(2,1)}), bf16[32,96,128]{2,1,0:T(8,128)(2,1)S(1)}, u32[]{:S(2)}, u32[]{:S(2)}) async-start(bf16[32,96,128]{2,1,0:T(8,128)(2,1)} %shard_map.102), calls=%async_computation | async-start | bytes 1572864 | tf_op jit(solution)/shard_map/all_to_all | solution.py:279
  125.0 8.8 %collective-permute-start.2 = (bf16[32,32,128]{2,1,0:T(8,128)(2,1)}, bf16[32,32,128]{2,1,0:T(8,128)(2,1)}, u32[]{:S(2)}, u32[]{:S(2)}) collective-permute-start(bf16[32,32,128]{2,1,0:T(8,128)(2,1)} %slice.18), channel_id=1, source_target_pairs={{0,96},{32,0},{64,32},{96,64},{128,224},{160,128},{192,160},{224,1... | collective-permute-start | bytes 786440 | tf_op jit(solution)/shard_map/ppermute | solution.py:282
  126.9 22.7 %collective-permute-start.1 = (bf16[32,32,128]{2,1,0:T(8,128)(2,1)}, bf16[32,32,128]{2,1,0:T(8,128)(2,1)}, u32[]{:S(2)}, u32[]{:S(2)}) collective-permute-start(bf16[32,32,128]{2,1,0:T(8,128)(2,1)} %slice.18), channel_id=1, source_target_pairs={{0,64},{32,96},{64,0},{96,32},{128,192},{160,224},{192,128},{224,1... | collective-permute-start | bytes 786440 | tf_op jit(solution)/shard_map/ppermute | solution.py:282
  128.8 20.8 %collective-permute-start = (bf16[32,32,128]{2,1,0:T(8,128)(2,1)}, bf16[32,32,128]{2,1,0:T(8,128)(2,1)}, u32[]{:S(2)}, u32[]{:S(2)}) collective-permute-start(bf16[32,32,128]{2,1,0:T(8,128)(2,1)} %slice.18), channel_id=1, source_target_pairs={{0,32},{32,64},{64,96},{96,0},{128,160},{160,192},{192,224},{224,1... | collective-permute-start | bytes 786440 | tf_op jit(solution)/shard_map/ppermute | solution.py:282
  162.0 26.9 %collective-permute-start.3 = (bf16[32,96,128]{2,1,0:T(8,128)(2,1)S(1)}, bf16[32,96,128]{2,1,0:T(8,128)(2,1)S(1)}, u32[]{:S(2)}, u32[]{:S(2)}) collective-permute-start(bf16[32,96,128]{2,1,0:T(8,128)(2,1)S(1)} %get-tuple-element.16), channel_id=1, source_target_pairs={{4,0},{8,4},{12,8},{16,12},{20,16},{24,20},{28,24},{36,32},{40,36}... | collective-permute-start | bytes 2359304 | tf_op jit(solution)/shard_map/ppermute | solution.py:295
  165.0 13.2 %collective-permute-start.4 = (bf16[32,32,128]{2,1,0:T(8,128)(2,1)S(1)}, bf16[32,32,128]{2,1,0:T(8,128)(2,1)S(1)}, u32[]{:S(2)}, u32[]{:S(2)}) collective-permute-start(bf16[32,32,128]{2,1,0:T(8,128)(2,1)S(1)} %get-tuple-element.17), channel_id=1, source_target_pairs={{4,32},{8,36},{12,40},{16,44},{20,48},{24,52},{28,56},{36,64},{40,... | collective-permute-start | bytes 786440 | tf_op jit(solution)/shard_map/ppermute | solution.py:295
  167.9 21.0 %collective-permute-start.5 = (bf16[32,32,128]{2,1,0:T(8,128)(2,1)S(1)}, bf16[32,32,128]{2,1,0:T(8,128)(2,1)S(1)}, u32[]{:S(2)}, u32[]{:S(2)}) collective-permute-start(bf16[32,32,128]{2,1,0:T(8,128)(2,1)S(1)} %get-tuple-element.18), channel_id=1, source_target_pairs={{4,64},{8,68},{12,72},{16,76},{20,80},{24,84},{28,88},{36,96},{40,... | collective-permute-start | bytes 786440 | tf_op jit(solution)/shard_map/ppermute | solution.py:295
  171.8 17.1 %collective-permute-start.6 = (bf16[32,32,128]{2,1,0:T(8,128)(2,1)S(1)}, bf16[32,32,128]{2,1,0:T(8,128)(2,1)S(1)}, u32[]{:S(2)}, u32[]{:S(2)}) collective-permute-start(bf16[32,32,128]{2,1,0:T(8,128)(2,1)S(1)} %get-tuple-element.19), channel_id=1, source_target_pairs={{4,96},{8,100},{12,104},{16,108},{20,112},{24,116},{28,120},{36,0}... | collective-permute-start | bytes 786440 | tf_op jit(solution)/shard_map/ppermute | solution.py:295
  190.0 99.7 %all-to-all-start.1 = ((bf16[32,96,128]{2,1,0:T(8,128)(2,1)}), bf16[32,96,128]{2,1,0:T(8,128)(2,1)S(1)}, u32[]{:S(2)}, u32[]{:S(2)}) async-start(bf16[32,96,128]{2,1,0:T(8,128)(2,1)} %shard_map.105), calls=%async_computation.1 | async-start | bytes 1572864 | tf_op jit(solution)/shard_map/all_to_all | solution.py:306
  201.3 39.4 %reduce-scatter.4.cloned.1.call-start = ((), (), s32[]{:S(2)}) async-start(), calls=%async_computation.3 | async-start | bytes 163840
Sparse Core Ops, SparseCore 0:
  206.1 34.5 reduce-scatter.3

commit v4 on v3

--- a/solution.py
+++ b/solution.py
@@ -96,9 +96,9 @@
 def main_kernel(
     place_ref, tiles_ref, live_ref, query_ref, recv_ref, *refs,
 ):
-    parts, table_ref, own_ref = refs[: GROUP - 1], refs[GROUP - 1], refs[GROUP]
-    outs, steps_ref = refs[GROUP + 1 : 2 * GROUP], refs[2 * GROUP]
-    kv, kt, acc, bias_acc, even, odd = refs[2 * GROUP + 1 :]
+    parts, table_ref, own_ref = refs[:GROUP], refs[GROUP], refs[GROUP + 1]
+    outs, steps_ref = refs[GROUP + 2 : 2 * GROUP + 1], refs[2 * GROUP + 1]
+    kv, kt, acc, bias_acc, even, odd = refs[2 * GROUP + 2 :]
     tiles_n = recv_ref.shape[0]
     scale = HD ** (-0.5)
     place = place_ref[0]
@@ -107,9 +107,11 @@
         return pl.ds(pl.multiple_of(lax.rem(j, GROUP) * QUART, QUART), QUART)
 
     def begin(b, carry):
+        across, below, above, passed = [part[b] for part in parts]
         kv[b, quarter(place), :] = recv_ref[b, HD:PACK, :]
-        for d in range(1, GROUP):
-            kv[b, quarter(place + GROUP - d), :] = parts[d - 1][b]
+        kv[b, quarter(place + 2), :] = across
+        kv[b, quarter(place + 3), :] = jnp.where(place == 0, passed, below)
+        kv[b, quarter(place + 1), :] = jnp.where(place == GROUP - 1, passed, above)
         kt[b] = kv[b].T[0:HD]
         bias_acc[b] = jnp.zeros((TILE, TILE), wide)
         return carry
@@ -226,7 +228,7 @@
             *[share] * (GROUP - 1),
             jax.ShapeDtypeStruct((tiles_n, 1, 2 * TILE), wide),
         ),
-        in_specs=[in_smem] * 3 + [in_vmem] * (GROUP + 2),
+        in_specs=[in_smem] * 3 + [in_vmem] * (GROUP + 3),
         out_specs=(in_vmem,) * (GROUP + 1),
         scratch_shapes=[
             pltpu.VMEM((tiles_n, TILE, 2 * HD), low),
@@ -279,7 +281,16 @@
     recv = lax.all_to_all(packed, "seq", split_axis=0, concat_axis=0, tiled=True)
     table = make_table(rel_bias[0, 0], tiles_n)
     quarters, table = lax.optimization_barrier((recv[:, HD:PACK, :], table))
-    parts = [lax.ppermute(quarters, "seq", passed_on(d)) for d in range(1, GROUP)]
+    starts = range(0, seq_n, GROUP)
+
+    def within(x, pairs):
+        return lax.ppermute(x, "seq", [(g + a, g + b) for g in starts for a, b in pairs])
+
+    across = within(quarters, [(0, 2), (1, 3), (2, 0), (3, 1)])
+    below = within(quarters, [(0, 1), (1, 2), (2, 3)])
+    above = within(quarters, [(1, 0), (2, 1), (3, 2)])
+    passed = within(across, [(1, 0), (2, 3)])
+    parts = (across, below, above, passed)
     place = (lax.axis_index("seq") % GROUP).astype(jnp.int32).reshape(1)
     own, *terms, steps = head_grads(
         place, key_tiles[0, 0], live_count[0, 0], saved_queries[0, 0].T, recv, parts, table

time: 298 us -> 295 us (0.990)
  the two profiles are of different devices: /device:TPU:15 before, /device:TPU:13 now
where the time goes in v4:
time: 295 us
  waiting for transfers between devices  199 us (67%)
  starting transfers between devices  58.9 us (20%)
  Pallas kernels  18 us (6%)
  between operations  14.2 us (5%)
  local copies, waits for them, and re-layouts  3.83 us (1%)
    all_to_all x2, waiting for transfers between devices, per_device(): lax.all_to_all(packed, 'seq', split_axis=0, concat_axis=0, tiled=True)  131 us
    unnamed x2, waiting for transfers between devices  38.4 us
    all_to_all x2, starting transfers between devices, per_device(): lax.all_to_all(packed, 'seq', split_axis=0, concat_axis=0, tiled=True)  37.1 us
    ppermute x4, waiting for transfers between devices, within(): lax.ppermute(x, 'seq', [(g + a, g + b) for g in starts for a, b in pairs])  15 us
    ppermute x4, waiting for transfers between devices, moved(): return lax.ppermute(x, ('seq', 'pipe'), pairs)  14.7 us
    ppermute x4, starting transfers between devices, moved(): return lax.ppermute(x, ('seq', 'pipe'), pairs)  12.5 us
    pallas_call x1, Pallas kernels, head_grads(): pl.pallas_call(main_kernel, out_shape=(jax.ShapeDtypeStruct((tiles_n, PAC...  12.5 us
    ppermute x4, starting transfers between devices, within(): lax.ppermute(x, 'seq', [(g + a, g + b) for g in starts for a, b in pairs])  9.19 us
  transfers between devices with their start and end apart: 11, of which 7 were waited for; matrix products, arithmetic and copies ran while one was open for 1% of the time, Pallas kernels for 0%

profile of v4, /device:TPU:13, one launch (start us, length us, event | category | flops | bytes accessed | tf_op | source)
XLA Modules:
  0.0 294.9 jit_solution(17175460176074326147)
XLA Ops:
  7.2 2.3 shard_map.102
  9.5 28.6 %all-to-all-start = ((bf16[32,96,128]{2,1,0:T(8,128)(2,1)}), bf16[32,96,128]{2,1,0:T(8,128)(2,1)S(1)}, u32[]{:S(2)}, u32[]{:S(2)}) async-start(bf16[32,96,128]{2,1,0:T(8,128)(2,1)} %shard_map.102), calls=%async_computation | async-start | bytes 1572864 | tf_op jit(solution)/shard_map/all_to_all | solution.py:281
  39.5 1.2 shard_map.103.refs_4_
  40.7 83.6 %all-to-all-done.recv_ref = bf16[32,96,128]{2,1,0:T(8,128)(2,1)S(1)} async-done(((bf16[32,96,128]{2,1,0:T(8,128)(2,1)}), bf16[32,96,128]{2,1,0:T(8,128)(2,1)S(1)}, u32[]{:S(2)}, u32[]{:S(2)}) %all-to-all-start) | async-done | bytes 786464 | tf_op jit(solution)/shard_map/all_to_all | solution.py:281
  125.0 1.9 collective-permute-start
  126.9 1.3 collective-permute-start.2
  128.2 4.7 %collective-permute-start.1 = (bf16[32,32,128]{2,1,0:T(8,128)(2,1)}, bf16[32,32,128]{2,1,0:T(8,128)(2,1)}, u32[]{:S(2)}, u32[]{:S(2)}) collective-permute-start(bf16[32,32,128]{2,1,0:T(8,128)(2,1)} %slice.18), channel_id=1, source_target_pairs={{0,32},{32,64},{64,96},{128,160},{160,192},{192,224},{256,288},{28... | collective-permute-start | bytes 786440 | tf_op jit(solution)/shard_map/ppermute | solution.py:287
  132.9 6.9 %collective-permute-done.refs_0_ = bf16[32,32,128]{2,1,0:T(8,128)(2,1)} collective-permute-done((bf16[32,32,128]{2,1,0:T(8,128)(2,1)}, bf16[32,32,128]{2,1,0:T(8,128)(2,1)}, u32[]{:S(2)}, u32[]{:S(2)}) %collective-permute-start) | collective-permute-done | bytes 262176 | tf_op jit(solution)/shard_map/ppermute | solution.py:287
  139.8 1.3 collective-permute-start.3
  141.2 8.1 %collective-permute-done.3.refs_3_ = bf16[32,32,128]{2,1,0:T(8,128)(2,1)} collective-permute-done((bf16[32,32,128]{2,1,0:T(8,128)(2,1)}, bf16[32,32,128]{2,1,0:T(8,128)(2,1)}, u32[]{:S(2)}, u32[]{:S(2)}) %collective-permute-start.3) | collective-permute-done | bytes 262176 | tf_op jit(solution)/shard_map/ppermute | solution.py:287
  149.3 12.5 %shard_map.104 = (bf16[32,96,128]{2,1,0:T(8,128)(2,1)S(1)}, bf16[32,32,128]{2,1,0:T(8,128)(2,1)S(1)}, bf16[32,32,128]{2,1,0:T(8,128)(2,1)S(1)}, bf16[32,32,128]{2,1,0:T(8,128)(2,1)S(1)}, f32[32,1,256]{2,1,0:T(1,128)S(1)}) custom-call(s32[1]{0:T(128)} %bitcast.2.place_ref, s32[32,4]{1,0:T(8,128)S(1)} %copy.19.tiles_ref, s32[32]{0:T(128)S(1)} %bitcast.25, ...), custom_call_target="tpu_custom_call" | custom-call | tf_op jit(solution)/shard_map/pallas_call | solution.py:224
  161.8 3.4 %collective-permute-start.4 = (bf16[32,96,128]{2,1,0:T(8,128)(2,1)S(1)}, bf16[32,96,128]{2,1,0:T(8,128)(2,1)S(1)}, u32[]{:S(2)}, u32[]{:S(2)}) collective-permute-start(bf16[32,96,128]{2,1,0:T(8,128)(2,1)S(1)} %get-tuple-element.16), channel_id=1, source_target_pairs={{4,0},{8,4},{12,8},{16,12},{20,16},{24,20},{28,24},{36,32},{40,36}... | collective-permute-start | bytes 2359304 | tf_op jit(solution)/shard_map/ppermute | solution.py:306
  165.2 1.9 collective-permute-start.5
  167.1 3.6 %collective-permute-start.6 = (bf16[32,32,128]{2,1,0:T(8,128)(2,1)S(1)}, bf16[32,32,128]{2,1,0:T(8,128)(2,1)S(1)}, u32[]{:S(2)}, u32[]{:S(2)}) collective-permute-start(bf16[32,32,128]{2,1,0:T(8,128)(2,1)S(1)} %get-tuple-element.18), channel_id=1, source_target_pairs={{4,64},{8,68},{12,72},{16,76},{20,80},{24,84},{28,88},{36,96},{40,... | collective-permute-start | bytes 786440 | tf_op jit(solution)/shard_map/ppermute | solution.py:306
  170.7 3.6 %collective-permute-start.7 = (bf16[32,32,128]{2,1,0:T(8,128)(2,1)S(1)}, bf16[32,32,128]{2,1,0:T(8,128)(2,1)S(1)}, u32[]{:S(2)}, u32[]{:S(2)}) collective-permute-start(bf16[32,32,128]{2,1,0:T(8,128)(2,1)S(1)} %get-tuple-element.19), channel_id=1, source_target_pairs={{4,96},{8,100},{12,104},{16,108},{20,112},{24,116},{28,120},{36,0}... | collective-permute-start | bytes 786440 | tf_op jit(solution)/shard_map/ppermute | solution.py:306
  174.4 4.0 %collective-permute-done.5.refs_0_ = bf16[32,32,128]{2,1,0:T(8,128)(2,1)S(1)} collective-permute-done((bf16[32,32,128]{2,1,0:T(8,128)(2,1)S(1)}, bf16[32,32,128]{2,1,0:T(8,128)(2,1)S(1)}, u32[]{:S(2)}, u32[]{:S(2)}) %collective-permute-start.5) | collective-permute-done | bytes 262176 | tf_op jit(solution)/shard_map/ppermute | solution.py:306
  178.4 10.7 %collective-permute-done.6.refs_1_ = bf16[32,32,128]{2,1,0:T(8,128)(2,1)S(1)} collective-permute-done((bf16[32,32,128]{2,1,0:T(8,128)(2,1)S(1)}, bf16[32,32,128]{2,1,0:T(8,128)(2,1)S(1)}, u32[]{:S(2)}, u32[]{:S(2)}) %collective-permute-start.6) | collective-permute-done | bytes 262176 | tf_op jit(solution)/shard_map/ppermute | solution.py:306
  189.1 1.1 shard_map.105
  190.2 8.5 %all-to-all-start.1 = ((bf16[32,96,128]{2,1,0:T(8,128)(2,1)}), bf16[32,96,128]{2,1,0:T(8,128)(2,1)S(1)}, u32[]{:S(2)}, u32[]{:S(2)}) async-start(bf16[32,96,128]{2,1,0:T(8,128)(2,1)} %shard_map.105), calls=%async_computation.1 | async-start | bytes 1572864 | tf_op jit(solution)/shard_map/all_to_all | solution.py:317
  199.0 0.8 copy.21
  199.8 38.4 %reduce-scatter.4.cloned.1.call-done = f32[64,1]{1,0:T(8,128)} async-done(((f32[256,1]{1,0:T(8,128)}), f32[64,1]{1,0:T(8,128)}) %reduce-scatter.4.cloned.1.call-update) | async-done | bytes 272
  238.2 1.3 copy.22
  239.6 47.4 %all-to-all-done.1.in_ref = bf16[32,96,128]{2,1,0:T(8,128)(2,1)S(1)} async-done(((bf16[32,96,128]{2,1,0:T(8,128)(2,1)}), bf16[32,96,128]{2,1,0:T(8,128)(2,1)S(1)}, u32[]{:S(2)}, u32[]{:S(2)}) %all-to-all-start.1) | async-done | bytes 786464 | tf_op jit(solution)/shard_map/all_to_all | solution.py:317
  287.0 1.1 shard_map.106
  (28 shorter events, 2.5 us)
Async XLA Ops:
  7.2 31.5 %copy-start.3 = (f32[1,1,256]{2,1,0:T(1,128)S(1)}, f32[1,1,256]{2,1,0:T(1,128)}, u32[]{:S(2)}) copy-start(f32[1,1,256]{2,1,0:T(1,128)} %param.11) | copy-start | bytes 3076
  9.5 131.7 %copy-start.2 = (s32[1,1,32,4]{2,3,1,0:T(4,128)S(1)}, s32[1,1,32,4]{2,3,1,0:T(4,128)}, u32[]{:S(2)}) copy-start(s32[1,1,32,4]{2,3,1,0:T(4,128)} %param.12) | copy-start | bytes 1540
  9.5 139.8 %copy-start = (bf16[1,1,4096,64]{2,3,1,0:T(8,128)(2,1)S(1)}, bf16[1,1,4096,64]{2,3,1,0:T(8,128)(2,1)}, u32[]{:S(2)}) copy-start(bf16[1,1,4096,64]{2,3,1,0:T(8,128)(2,1)} %param.7) | copy-start | bytes 1572868
  9.5 139.8 %copy-start.1 = (s32[1,1,32]{2,1,0:T(1,128)S(1)}, s32[1,1,32]{2,1,0:T(1,128)}, u32[]{:S(2)}) copy-start(s32[1,1,32]{2,1,0:T(1,128)} %param.13) | copy-start | bytes 388
  9.5 114.7 %all-to-all-start = ((bf16[32,96,128]{2,1,0:T(8,128)(2,1)}), bf16[32,96,128]{2,1,0:T(8,128)(2,1)S(1)}, u32[]{:S(2)}, u32[]{:S(2)}) async-start(bf16[32,96,128]{2,1,0:T(8,128)(2,1)} %shard_map.102), calls=%async_computation | async-start | bytes 1572864 | tf_op jit(solution)/shard_map/all_to_all | solution.py:281
  125.0 14.9 %collective-permute-start = (bf16[32,32,128]{2,1,0:T(8,128)(2,1)}, bf16[32,32,128]{2,1,0:T(8,128)(2,1)}, u32[]{:S(2)}, u32[]{:S(2)}) collective-permute-start(bf16[32,32,128]{2,1,0:T(8,128)(2,1)} %slice.18), channel_id=1, source_target_pairs={{0,64},{32,96},{64,0},{96,32},{128,192},{160,224},{192,128},{224,1... | collective-permute-start | bytes 786440 | tf_op jit(solution)/shard_map/ppermute | solution.py:287
  126.9 14.4 %collective-permute-start.2 = (bf16[32,32,128]{2,1,0:T(8,128)(2,1)}, bf16[32,32,128]{2,1,0:T(8,128)(2,1)}, u32[]{:S(2)}, u32[]{:S(2)}) collective-permute-start(bf16[32,32,128]{2,1,0:T(8,128)(2,1)} %slice.18), channel_id=1, source_target_pairs={{32,0},{64,32},{96,64},{160,128},{192,160},{224,192},{288,256},{32... | collective-permute-start | bytes 786440 | tf_op jit(solution)/shard_map/ppermute | solution.py:287
  128.2 13.1 %collective-permute-start.1 = (bf16[32,32,128]{2,1,0:T(8,128)(2,1)}, bf16[32,32,128]{2,1,0:T(8,128)(2,1)}, u32[]{:S(2)}, u32[]{:S(2)}) collective-permute-start(bf16[32,32,128]{2,1,0:T(8,128)(2,1)} %slice.18), channel_id=1, source_target_pairs={{0,32},{32,64},{64,96},{128,160},{160,192},{192,224},{256,288},{28... | collective-permute-start | bytes 786440 | tf_op jit(solution)/shard_map/ppermute | solution.py:287
  139.8 9.5 %collective-permute-start.3 = (bf16[32,32,128]{2,1,0:T(8,128)(2,1)}, bf16[32,32,128]{2,1,0:T(8,128)(2,1)}, u32[]{:S(2)}, u32[]{:S(2)}) collective-permute-start(bf16[32,32,128]{2,1,0:T(8,128)(2,1)} %collective-permute-done.refs_0_), channel_id=1, source_target_pairs={{32,0},{64,96},{160,128},{192,224},{288,256},{320,352},{416,384},{... | collective-permute-start | bytes 786440 | tf_op jit(solution)/shard_map/ppermute | solution.py:287
  161.8 27.3 %collective-permute-start.4 = (bf16[32,96,128]{2,1,0:T(8,128)(2,1)S(1)}, bf16[32,96,128]{2,1,0:T(8,128)(2,1)S(1)}, u32[]{:S(2)}, u32[]{:S(2)}) collective-permute-start(bf16[32,96,128]{2,1,0:T(8,128)(2,1)S(1)} %get-tuple-element.16), channel_id=1, source_target_pairs={{4,0},{8,4},{12,8},{16,12},{20,16},{24,20},{28,24},{36,32},{40,36}... | collective-permute-start | bytes 2359304 | tf_op jit(solution)/shard_map/ppermute | solution.py:306
  165.2 13.2 %collective-permute-start.5 = (bf16[32,32,128]{2,1,0:T(8,128)(2,1)S(1)}, bf16[32,32,128]{2,1,0:T(8,128)(2,1)S(1)}, u32[]{:S(2)}, u32[]{:S(2)}) collective-permute-start(bf16[32,32,128]{2,1,0:T(8,128)(2,1)S(1)} %get-tuple-element.17), channel_id=1, source_target_pairs={{4,32},{8,36},{12,40},{16,44},{20,48},{24,52},{28,56},{36,64},{40,... | collective-permute-start | bytes 786440 | tf_op jit(solution)/shard_map/ppermute | solution.py:306
  167.1 22.0 %collective-permute-start.6 = (bf16[32,32,128]{2,1,0:T(8,128)(2,1)S(1)}, bf16[32,32,128]{2,1,0:T(8,128)(2,1)S(1)}, u32[]{:S(2)}, u32[]{:S(2)}) collective-permute-start(bf16[32,32,128]{2,1,0:T(8,128)(2,1)S(1)} %get-tuple-element.18), channel_id=1, source_target_pairs={{4,64},{8,68},{12,72},{16,76},{20,80},{24,84},{28,88},{36,96},{40,... | collective-permute-start | bytes 786440 | tf_op jit(solution)/shard_map/ppermute | solution.py:306
  170.7 18.4 %collective-permute-start.7 = (bf16[32,32,128]{2,1,0:T(8,128)(2,1)S(1)}, bf16[32,32,128]{2,1,0:T(8,128)(2,1)S(1)}, u32[]{:S(2)}, u32[]{:S(2)}) collective-permute-start(bf16[32,32,128]{2,1,0:T(8,128)(2,1)S(1)} %get-tuple-element.19), channel_id=1, source_target_pairs={{4,96},{8,100},{12,104},{16,108},{20,112},{24,116},{28,120},{36,0}... | collective-permute-start | bytes 786440 | tf_op jit(solution)/shard_map/ppermute | solution.py:306
  190.2 96.8 %all-to-all-start.1 = ((bf16[32,96,128]{2,1,0:T(8,128)(2,1)}), bf16[32,96,128]{2,1,0:T(8,128)(2,1)S(1)}, u32[]{:S(2)}, u32[]{:S(2)}) async-start(bf16[32,96,128]{2,1,0:T(8,128)(2,1)} %shard_map.105), calls=%async_computation.1 | async-start | bytes 1572864 | tf_op jit(solution)/shard_map/all_to_all | solution.py:317
  198.7 39.5 %reduce-scatter.4.cloned.1.call-start = ((), (), s32[]{:S(2)}) async-start(), calls=%async_computation.3 | async-start | bytes 163840
Sparse Core Ops, SparseCore 0:
  203.5 34.7 reduce-scatter.3

commit v5 on v4

--- a/solution.py
+++ b/solution.py
@@ -14,6 +14,7 @@
 GROUP = HEADS // KVH
 QUART = TILE // GROUP
 PACK = HD + QUART
+ALONG = (2, 1, 3)
 
 neg_big = -1e30
 log2_e = 1.4426950408889634
@@ -69,8 +70,8 @@
         value_ref[:, at] = jnp.concatenate([s[:, HD : 2 * HD] for s in sides], axis=1)
 
 
-def sum_kernel(own_ref, *refs):
-    terms, out_ref = refs[:-1], refs[-1]
+def sum_kernel(*refs):
+    terms, own_ref, out_ref = refs[:-2], refs[-2], refs[-1]
     out_ref[:, 0:HD, :] = own_ref[:, 0:HD, :]
     total = own_ref[:, HD:PACK, :].astype(wide)
     for term in terms:
@@ -96,8 +97,8 @@
 def main_kernel(
     place_ref, tiles_ref, live_ref, query_ref, recv_ref, *refs,
 ):
-    parts, table_ref, own_ref = refs[:GROUP], refs[GROUP], refs[GROUP + 1]
-    outs, steps_ref = refs[GROUP + 2 : 2 * GROUP + 1], refs[2 * GROUP + 1]
+    parts, table_ref, outs = refs[:GROUP], refs[GROUP], refs[GROUP + 1 : 2 * GROUP]
+    own_ref, steps_ref = refs[2 * GROUP : 2 * GROUP + 2]
     kv, kt, acc, bias_acc, even, odd = refs[2 * GROUP + 2 :]
     tiles_n = recv_ref.shape[0]
     scale = HD ** (-0.5)
@@ -192,8 +193,8 @@
 
     def end(b, carry):
         own_ref[b, HD:PACK, :] = (acc[b, quarter(place), :] * sizes).astype(low)
-        for d in range(1, GROUP):
-            outs[d - 1][b] = (acc[b, quarter(place + d), :] * sizes).astype(low)
+        for d, out in zip(ALONG, outs):
+            out[b] = (acc[b, quarter(place + d), :] * sizes).astype(low)
         padded = jnp.concatenate([bias_acc[b], blank_right], axis=1)
         lined = padded[0:BUCKET]
         for step in range(1, TILE // BUCKET):
@@ -224,8 +225,8 @@
     return pl.pallas_call(
         main_kernel,
         out_shape=(
+            *[share] * (GROUP - 1),
             jax.ShapeDtypeStruct((tiles_n, PACK, TILE), low),
-            *[share] * (GROUP - 1),
             jax.ShapeDtypeStruct((tiles_n, 1, 2 * TILE), wide),
         ),
         in_specs=[in_smem] * 3 + [in_vmem] * (GROUP + 3),
@@ -292,7 +293,7 @@
     passed = within(across, [(1, 0), (2, 3)])
     parts = (across, below, above, passed)
     place = (lax.axis_index("seq") % GROUP).astype(jnp.int32).reshape(1)
-    own, *terms, steps = head_grads(
+    *terms, own, steps = head_grads(
         place, key_tiles[0, 0], live_count[0, 0], saved_queries[0, 0].T, recv, parts, table
     )
     bias_share = lax.psum_scatter(bias_row_of(steps), "dp", scatter_dimension=1, tiled=True)
@@ -305,7 +306,7 @@
         ]
         return lax.ppermute(x, ("seq", "pipe"), pairs)
 
-    terms = [moved(x, d) for d, x in enumerate(terms, 1)]
+    terms = [moved(x, d) for d, x in zip(ALONG, terms)]
     own = moved(own, 0)
     packed = pl.pallas_call(
         sum_kernel,
@@ -313,7 +314,7 @@
         in_specs=[in_vmem] * GROUP,
         out_specs=in_vmem,
         compiler_params=params(16),
-    )(own, *terms)
+    )(*terms, own)
     back_in = lax.all_to_all(packed, "seq", split_axis=0, concat_axis=0, tiled=True)
     sent_query, sent_keys, sent_values = pl.pallas_call(
         unpack_kernel,

time: 295 us -> 294 us (level)
  the two profiles are of different devices: /device:TPU:13 before, /device:TPU:11 now
where the time goes in v5:
time: 294 us
  waiting for transfers between devices  203 us (69%)
  starting transfers between devices  54.5 us (19%)
  Pallas kernels  18 us (6%)
  between operations  14.2 us (5%)
  local copies, waits for them, and re-layouts  3.83 us (1%)
    all_to_all x2, waiting for transfers between devices, per_device(): lax.all_to_all(packed, 'seq', split_axis=0, concat_axis=0, tiled=True)  131 us
    unnamed x2, waiting for transfers between devices  38.3 us
    all_to_all x2, starting transfers between devices, per_device(): lax.all_to_all(packed, 'seq', split_axis=0, concat_axis=0, tiled=True)  32.7 us
    ppermute x4, waiting for transfers between devices, moved(): return lax.ppermute(x, ('seq', 'pipe'), pairs)  18.2 us
    ppermute x4, waiting for transfers between devices, within(): lax.ppermute(x, 'seq', [(g + a, g + b) for g in starts for a, b in pairs])  15 us
    ppermute x4, starting transfers between devices, moved(): return lax.ppermute(x, ('seq', 'pipe'), pairs)  12.5 us
    pallas_call x1, Pallas kernels, head_grads(): pl.pallas_call(main_kernel, out_shape=(*[share] * (GROUP - 1), jax.ShapeD...  12.5 us
    ppermute x4, starting transfers between devices, within(): lax.ppermute(x, 'seq', [(g + a, g + b) for g in starts for a, b in pairs])  9.19 us
  transfers between devices with their start and end apart: 11, of which 7 were waited for; matrix products, arithmetic and copies ran while one was open for 1% of the time, Pallas kernels for 0%

profile of v5, /device:TPU:11, one launch (start us, length us, event | category | flops | bytes accessed | tf_op | source)
XLA Modules:
  0.0 293.9 jit_solution(6809347990459256978)
XLA Ops:
  7.2 2.3 shard_map.102
  9.5 28.6 %all-to-all-start = ((bf16[32,96,128]{2,1,0:T(8,128)(2,1)}), bf16[32,96,128]{2,1,0:T(8,128)(2,1)S(1)}, u32[]{:S(2)}, u32[]{:S(2)}) async-start(bf16[32,96,128]{2,1,0:T(8,128)(2,1)} %shard_map.102), calls=%async_computation | async-start | bytes 1572864 | tf_op jit(solution)/shard_map/all_to_all | solution.py:282
  39.5 1.2 shard_map.103.refs_4_
  40.7 83.6 %all-to-all-done.recv_ref = bf16[32,96,128]{2,1,0:T(8,128)(2,1)S(1)} async-done(((bf16[32,96,128]{2,1,0:T(8,128)(2,1)}), bf16[32,96,128]{2,1,0:T(8,128)(2,1)S(1)}, u32[]{:S(2)}, u32[]{:S(2)}) %all-to-all-start) | async-done | bytes 786464 | tf_op jit(solution)/shard_map/all_to_all | solution.py:282
  125.0 1.9 collective-permute-start
  126.9 1.3 collective-permute-start.2
  128.2 4.7 %collective-permute-start.1 = (bf16[32,32,128]{2,1,0:T(8,128)(2,1)}, bf16[32,32,128]{2,1,0:T(8,128)(2,1)}, u32[]{:S(2)}, u32[]{:S(2)}) collective-permute-start(bf16[32,32,128]{2,1,0:T(8,128)(2,1)} %slice.18), channel_id=1, source_target_pairs={{0,32},{32,64},{64,96},{128,160},{160,192},{192,224},{256,288},{28... | collective-permute-start | bytes 786440 | tf_op jit(solution)/shard_map/ppermute | solution.py:288
  132.9 6.9 %collective-permute-done.refs_0_ = bf16[32,32,128]{2,1,0:T(8,128)(2,1)} collective-permute-done((bf16[32,32,128]{2,1,0:T(8,128)(2,1)}, bf16[32,32,128]{2,1,0:T(8,128)(2,1)}, u32[]{:S(2)}, u32[]{:S(2)}) %collective-permute-start) | collective-permute-done | bytes 262176 | tf_op jit(solution)/shard_map/ppermute | solution.py:288
  139.8 1.3 collective-permute-start.3
  141.2 8.1 %collective-permute-done.3.refs_3_ = bf16[32,32,128]{2,1,0:T(8,128)(2,1)} collective-permute-done((bf16[32,32,128]{2,1,0:T(8,128)(2,1)}, bf16[32,32,128]{2,1,0:T(8,128)(2,1)}, u32[]{:S(2)}, u32[]{:S(2)}) %collective-permute-start.3) | collective-permute-done | bytes 262176 | tf_op jit(solution)/shard_map/ppermute | solution.py:288
  149.3 12.5 %shard_map.104 = (bf16[32,32,128]{2,1,0:T(8,128)(2,1)S(1)}, bf16[32,32,128]{2,1,0:T(8,128)(2,1)S(1)}, bf16[32,32,128]{2,1,0:T(8,128)(2,1)S(1)}, bf16[32,96,128]{2,1,0:T(8,128)(2,1)S(1)}, f32[32,1,256]{2,1,0:T(1,128)S(1)}) custom-call(s32[1]{0:T(128)} %bitcast.2.place_ref, s32[32,4]{1,0:T(8,128)S(1)} %copy.19.tiles_ref, s32[32]{0:T(128)S(1)} %bitcast.25, ...), custom_call_target="tpu_custom_call" | custom-call | tf_op jit(solution)/shard_map/pallas_call | solution.py:225
  161.8 3.3 %collective-permute-start.7 = (bf16[32,96,128]{2,1,0:T(8,128)(2,1)S(1)}, bf16[32,96,128]{2,1,0:T(8,128)(2,1)S(1)}, u32[]{:S(2)}, u32[]{:S(2)}) collective-permute-start(bf16[32,96,128]{2,1,0:T(8,128)(2,1)S(1)} %get-tuple-element.19), channel_id=1, source_target_pairs={{4,0},{8,4},{12,8},{16,12},{20,16},{24,20},{28,24},{36,32},{40,36}... | collective-permute-start | bytes 2359304 | tf_op jit(solution)/shard_map/ppermute | solution.py:307
  165.2 1.9 collective-permute-start.4
  167.1 3.6 %collective-permute-start.5 = (bf16[32,32,128]{2,1,0:T(8,128)(2,1)S(1)}, bf16[32,32,128]{2,1,0:T(8,128)(2,1)S(1)}, u32[]{:S(2)}, u32[]{:S(2)}) collective-permute-start(bf16[32,32,128]{2,1,0:T(8,128)(2,1)S(1)} %get-tuple-element.17), channel_id=1, source_target_pairs={{4,32},{8,36},{12,40},{16,44},{20,48},{24,52},{28,56},{36,64},{40,... | collective-permute-start | bytes 786440 | tf_op jit(solution)/shard_map/ppermute | solution.py:307
  170.7 3.6 %collective-permute-start.6 = (bf16[32,32,128]{2,1,0:T(8,128)(2,1)S(1)}, bf16[32,32,128]{2,1,0:T(8,128)(2,1)S(1)}, u32[]{:S(2)}, u32[]{:S(2)}) collective-permute-start(bf16[32,32,128]{2,1,0:T(8,128)(2,1)S(1)} %get-tuple-element.18), channel_id=1, source_target_pairs={{4,96},{8,100},{12,104},{16,108},{20,112},{24,116},{28,120},{36,0}... | collective-permute-start | bytes 786440 | tf_op jit(solution)/shard_map/ppermute | solution.py:307
  174.4 12.9 %collective-permute-done.4.refs_0_ = bf16[32,32,128]{2,1,0:T(8,128)(2,1)S(1)} collective-permute-done((bf16[32,32,128]{2,1,0:T(8,128)(2,1)S(1)}, bf16[32,32,128]{2,1,0:T(8,128)(2,1)S(1)}, u32[]{:S(2)}, u32[]{:S(2)}) %collective-permute-start.4) | collective-permute-done | bytes 262176 | tf_op jit(solution)/shard_map/ppermute | solution.py:307
  187.3 5.3 %collective-permute-done.6.refs_2_ = bf16[32,32,128]{2,1,0:T(8,128)(2,1)S(1)} collective-permute-done((bf16[32,32,128]{2,1,0:T(8,128)(2,1)S(1)}, bf16[32,32,128]{2,1,0:T(8,128)(2,1)S(1)}, u32[]{:S(2)}, u32[]{:S(2)}) %collective-permute-start.6) | collective-permute-done | bytes 262176 | tf_op jit(solution)/shard_map/ppermute | solution.py:307
  192.5 1.0 shard_map.105
  193.6 4.1 %all-to-all-start.1 = ((bf16[32,96,128]{2,1,0:T(8,128)(2,1)}), bf16[32,96,128]{2,1,0:T(8,128)(2,1)S(1)}, u32[]{:S(2)}, u32[]{:S(2)}) async-start(bf16[32,96,128]{2,1,0:T(8,128)(2,1)} %shard_map.105), calls=%async_computation.1 | async-start | bytes 1572864 | tf_op jit(solution)/shard_map/all_to_all | solution.py:318
  198.0 0.8 copy.21
  198.8 38.3 %reduce-scatter.4.cloned.1.call-done = f32[64,1]{1,0:T(8,128)} async-done(((f32[256,1]{1,0:T(8,128)}), f32[64,1]{1,0:T(8,128)}) %reduce-scatter.4.cloned.1.call-update) | async-done | bytes 272
  237.1 1.3 copy.22
  238.5 47.5 %all-to-all-done.1.in_ref = bf16[32,96,128]{2,1,0:T(8,128)(2,1)S(1)} async-done(((bf16[32,96,128]{2,1,0:T(8,128)(2,1)}), bf16[32,96,128]{2,1,0:T(8,128)(2,1)S(1)}, u32[]{:S(2)}, u32[]{:S(2)}) %all-to-all-start.1) | async-done | bytes 786464 | tf_op jit(solution)/shard_map/all_to_all | solution.py:318
  286.0 1.1 shard_map.106
  (28 shorter events, 2.5 us)
Async XLA Ops:
  7.2 31.5 %copy-start.3 = (f32[1,1,256]{2,1,0:T(1,128)S(1)}, f32[1,1,256]{2,1,0:T(1,128)}, u32[]{:S(2)}) copy-start(f32[1,1,256]{2,1,0:T(1,128)} %param.11) | copy-start | bytes 3076
  9.5 131.7 %copy-start.2 = (s32[1,1,32,4]{2,3,1,0:T(4,128)S(1)}, s32[1,1,32,4]{2,3,1,0:T(4,128)}, u32[]{:S(2)}) copy-start(s32[1,1,32,4]{2,3,1,0:T(4,128)} %param.12) | copy-start | bytes 1540
  9.5 139.8 %copy-start = (bf16[1,1,4096,64]{2,3,1,0:T(8,128)(2,1)S(1)}, bf16[1,1,4096,64]{2,3,1,0:T(8,128)(2,1)}, u32[]{:S(2)}) copy-start(bf16[1,1,4096,64]{2,3,1,0:T(8,128)(2,1)} %param.7) | copy-start | bytes 1572868
  9.5 139.8 %copy-start.1 = (s32[1,1,32]{2,1,0:T(1,128)S(1)}, s32[1,1,32]{2,1,0:T(1,128)}, u32[]{:S(2)}) copy-start(s32[1,1,32]{2,1,0:T(1,128)} %param.13) | copy-start | bytes 388
  9.5 114.7 %all-to-all-start = ((bf16[32,96,128]{2,1,0:T(8,128)(2,1)}), bf16[32,96,128]{2,1,0:T(8,128)(2,1)S(1)}, u32[]{:S(2)}, u32[]{:S(2)}) async-start(bf16[32,96,128]{2,1,0:T(8,128)(2,1)} %shard_map.102), calls=%async_computation | async-start | bytes 1572864 | tf_op jit(solution)/shard_map/all_to_all | solution.py:282
  125.0 14.9 %collective-permute-start = (bf16[32,32,128]{2,1,0:T(8,128)(2,1)}, bf16[32,32,128]{2,1,0:T(8,128)(2,1)}, u32[]{:S(2)}, u32[]{:S(2)}) collective-permute-start(bf16[32,32,128]{2,1,0:T(8,128)(2,1)} %slice.18), channel_id=1, source_target_pairs={{0,64},{32,96},{64,0},{96,32},{128,192},{160,224},{192,128},{224,1... | collective-permute-start | bytes 786440 | tf_op jit(solution)/shard_map/ppermute | solution.py:288
  126.9 14.4 %collective-permute-start.2 = (bf16[32,32,128]{2,1,0:T(8,128)(2,1)}, bf16[32,32,128]{2,1,0:T(8,128)(2,1)}, u32[]{:S(2)}, u32[]{:S(2)}) collective-permute-start(bf16[32,32,128]{2,1,0:T(8,128)(2,1)} %slice.18), channel_id=1, source_target_pairs={{32,0},{64,32},{96,64},{160,128},{192,160},{224,192},{288,256},{32... | collective-permute-start | bytes 786440 | tf_op jit(solution)/shard_map/ppermute | solution.py:288
  128.2 13.1 %collective-permute-start.1 = (bf16[32,32,128]{2,1,0:T(8,128)(2,1)}, bf16[32,32,128]{2,1,0:T(8,128)(2,1)}, u32[]{:S(2)}, u32[]{:S(2)}) collective-permute-start(bf16[32,32,128]{2,1,0:T(8,128)(2,1)} %slice.18), channel_id=1, source_target_pairs={{0,32},{32,64},{64,96},{128,160},{160,192},{192,224},{256,288},{28... | collective-permute-start | bytes 786440 | tf_op jit(solution)/shard_map/ppermute | solution.py:288
  139.8 9.5 %collective-permute-start.3 = (bf16[32,32,128]{2,1,0:T(8,128)(2,1)}, bf16[32,32,128]{2,1,0:T(8,128)(2,1)}, u32[]{:S(2)}, u32[]{:S(2)}) collective-permute-start(bf16[32,32,128]{2,1,0:T(8,128)(2,1)} %collective-permute-done.refs_0_), channel_id=1, source_target_pairs={{32,0},{64,96},{160,128},{192,224},{288,256},{320,352},{416,384},{... | collective-permute-start | bytes 786440 | tf_op jit(solution)/shard_map/ppermute | solution.py:288
  161.8 30.7 %collective-permute-start.7 = (bf16[32,96,128]{2,1,0:T(8,128)(2,1)S(1)}, bf16[32,96,128]{2,1,0:T(8,128)(2,1)S(1)}, u32[]{:S(2)}, u32[]{:S(2)}) collective-permute-start(bf16[32,96,128]{2,1,0:T(8,128)(2,1)S(1)} %get-tuple-element.19), channel_id=1, source_target_pairs={{4,0},{8,4},{12,8},{16,12},{20,16},{24,20},{28,24},{36,32},{40,36}... | collective-permute-start | bytes 2359304 | tf_op jit(solution)/shard_map/ppermute | solution.py:307
  165.2 22.1 %collective-permute-start.4 = (bf16[32,32,128]{2,1,0:T(8,128)(2,1)S(1)}, bf16[32,32,128]{2,1,0:T(8,128)(2,1)S(1)}, u32[]{:S(2)}, u32[]{:S(2)}) collective-permute-start(bf16[32,32,128]{2,1,0:T(8,128)(2,1)S(1)} %get-tuple-element.16), channel_id=1, source_target_pairs={{4,64},{8,68},{12,72},{16,76},{20,80},{24,84},{28,88},{36,96},{40,... | collective-permute-start | bytes 786440 | tf_op jit(solution)/shard_map/ppermute | solution.py:307
  167.1 20.2 %collective-permute-start.5 = (bf16[32,32,128]{2,1,0:T(8,128)(2,1)S(1)}, bf16[32,32,128]{2,1,0:T(8,128)(2,1)S(1)}, u32[]{:S(2)}, u32[]{:S(2)}) collective-permute-start(bf16[32,32,128]{2,1,0:T(8,128)(2,1)S(1)} %get-tuple-element.17), channel_id=1, source_target_pairs={{4,32},{8,36},{12,40},{16,44},{20,48},{24,52},{28,56},{36,64},{40,... | collective-permute-start | bytes 786440 | tf_op jit(solution)/shard_map/ppermute | solution.py:307
  170.7 21.8 %collective-permute-start.6 = (bf16[32,32,128]{2,1,0:T(8,128)(2,1)S(1)}, bf16[32,32,128]{2,1,0:T(8,128)(2,1)S(1)}, u32[]{:S(2)}, u32[]{:S(2)}) collective-permute-start(bf16[32,32,128]{2,1,0:T(8,128)(2,1)S(1)} %get-tuple-element.18), channel_id=1, source_target_pairs={{4,96},{8,100},{12,104},{16,108},{20,112},{24,116},{28,120},{36,0}... | collective-permute-start | bytes 786440 | tf_op jit(solution)/shard_map/ppermute | solution.py:307
  193.6 92.4 %all-to-all-start.1 = ((bf16[32,96,128]{2,1,0:T(8,128)(2,1)}), bf16[32,96,128]{2,1,0:T(8,128)(2,1)S(1)}, u32[]{:S(2)}, u32[]{:S(2)}) async-start(bf16[32,96,128]{2,1,0:T(8,128)(2,1)} %shard_map.105), calls=%async_computation.1 | async-start | bytes 1572864 | tf_op jit(solution)/shard_map/all_to_all | solution.py:318
  197.7 39.5 %reduce-scatter.4.cloned.1.call-start = ((), (), s32[]{:S(2)}) async-start(), calls=%async_computation.3 | async-start | bytes 163840
Sparse Core Ops, SparseCore 0:
  202.5 34.6 reduce-scatter.3
